TPU v7x, 32 devices: a whole 2x2x4 slice. The times are simulated.
32 devices in a mesh: blk: 8 (over y, x, core), grp: 4 (over z).
Axes of the slice: x: 2, y: 2, z: 4, core: 2. Of those that a mesh axis runs over, the one named last changes fastest.
Arguments:
- blocks: bfloat16 [64, 12, 128, 128], P(('blk', 'grp')), may hold values from -0.5 to 0.5
- neighbours: int32 [64, 12], P(('blk', 'grp')), may hold values from 0 to 9
- tentative: bfloat16 [64, 128, 128], P(('blk', 'grp')), may hold values from -0.5 to 0.5
- inv_diag: float32 [64, 128], P(('blk', 'grp')), may hold values from 0.5 to 2
- coarse_map: int32 [8, 4, 2], P(None, 'grp'), may hold values from 0 to 1
- counts: int32 [32], P(('blk', 'grp')), may hold values from 1 to 2, as said below
Outputs:
- coarse: float32 [16, 5, 2, 128, 128], P('blk', None, None, 'grp')
Inputs may be any that keep to these rules, and one draw needn't show every extreme that they name: `counts`: each device's set holds 1 or 2 live rows; at least one device holds 2.
All inputs are finite; a program needn't handle non-finite values.
Results may differ from a plain program's by a relative error of at most 0.0034.
Values may be sent and summed in bfloat16 or wider, within the bound.
No kernel may reach another device: no remote copies, remote signals or barrier semaphores. Data moves between devices by JAX's collectives and lax.ppermute only.
A program may use at most 64 MiB of HBM per device.

v0:
```python
import jax
import jax.numpy as jnp
from jax import lax
from jax.sharding import PartitionSpec as P

NCG = 2


omega = 0.6


def from_behind(block, axis, distance):
    devices = range(lax.axis_size(axis))
    route = [((i - distance) % len(devices), i) for i in devices]
    return lax.ppermute(block, axis, route)


def panel_pool(panels):
    near = [from_behind(panels, "blk", step) for step in (1, -1)]
    far = [from_behind(panels, "blk", step) for step in (2, -2)]
    return jnp.concatenate([far[0], near[0], panels, near[1], far[1]], axis=0)


def local(blocks, neighbours, tentative, inv_diag, coarse_map, counts):
    slot_count = tentative.shape[0]
    live_count = counts[0]
    live_rows = (jnp.arange(slot_count, dtype=jnp.int32) < live_count)[:, None, None]
    masked = jnp.where(live_rows, tentative, jnp.zeros_like(tentative))
    cycle_size = lax.axis_size("blk")
    here_index = lax.axis_index("blk")
    group_maps = coarse_map[:, 0, :]
    window = jnp.concatenate(
        [
            lax.dynamic_index_in_dim(
                group_maps, (here_index + offset) % cycle_size, 0, keepdims=True
            )
            for offset in (-2, -1, 0, 1, 2)
        ],
        axis=0,
    ).reshape(-1)
    own_map = window[2 * slot_count : 3 * slot_count]
    neighbour_map = window[neighbours]
    reach_index = neighbours // slot_count
    same_block = (reach_index == 2) & (neighbour_map == own_map[:, None])
    picked = masked[neighbours % slot_count]
    picked = jnp.where(same_block[:, :, None, None], picked, jnp.zeros_like(picked))
    smoothing = jnp.einsum("snij,snjk->sik", blocks, picked, preferred_element_type=jnp.float32)
    prolong = jnp.where(
        live_rows,
        tentative.astype(jnp.float32) - omega * inv_diag[:, :, None] * smoothing,
        jnp.float32(0.0),
    ).astype(jnp.bfloat16)
    gathered = panel_pool(prolong)
    dest_index = (own_map[:, None] * 5 + reach_index) * NCG + neighbour_map
    col_width = prolong.shape[2]
    targets = jnp.arange(NCG * 5 * NCG, dtype=jnp.int32)
    pair = jnp.einsum(
        "snij,snjk->snik", blocks, gathered[neighbours], preferred_element_type=jnp.float32
    ).astype(jnp.bfloat16)
    galerkin = jnp.einsum("sik,snij->snkj", prolong, pair, preferred_element_type=jnp.float32)
    onehot = (dest_index.reshape(-1)[None, :] == targets[:, None]).astype(jnp.float32)
    partial_sums = jnp.dot(
        onehot, galerkin.reshape(-1, col_width * col_width), precision=lax.Precision.HIGHEST
    )
    partial_sums = partial_sums.reshape(NCG, 5, NCG, col_width, col_width)
    return lax.psum_scatter(partial_sums, "grp", scatter_dimension=3, tiled=True)


def solution(mesh):
    return jax.shard_map(
        local,
        mesh=mesh,
        in_specs=(
            P(("blk", "grp"), None, None, None),
            P(("blk", "grp"), None),
            P(("blk", "grp"), None, None),
            P(("blk", "grp"), None),
            P(None, "grp", None),
            P(("blk", "grp")),
        ),
        out_specs=P("blk", None, None, "grp", None),
        check_vma=False,
    )
```

profile of v0, /device:TPU:0, one launch (start us, length us, event | category | flops | bytes accessed | tf_op | source)
XLA Modules:
  0.0 103.3 jit_solution(5564936460908952803)
XLA Ops:
  6.5 0.0 copy-start
  6.5 0.0 all-reduce.3.cloned.1.call-start
  6.5 1.1 %fusion.20 = (s32[2]{0:T(128)S(1)}, s32[2]{0:T(128)S(1)}, s32[2]{0:T(128)S(1)}, s32[2]{0:T(128)S(1)}, s32[2]{0:T(128)S(1)}) fusion(s32[8,1,2]{0,2,1:T(2,128)} %param.10, s32[]{:T(128)S(6)} %select_n.79, s32[]{:T(128)S(6)} %select_n.75, s32[]{:T(128)S(6)} %select_n.73, s32[]{:T(128)S(6)} %select_n.70, s32[]{:T(128)S(6)} %select_n.77), kind=kLoop, calls=%fused_computation.49 | loop fusion | bytes 100 | tf_op jit(solution)/shard_map/jit(dynamic_index_in_dim)/dynamic_slice | solution.py:34
  7.7 0.1 reshape.54
  7.8 0.7 add_select_fusion
  8.5 0.1 reshape.58
  8.5 0.7 gather_fusion
  9.2 0.1 reshape.57
  9.3 0.8 multiply_add_fusion.1
  10.1 0.1 reshape.66
  10.2 0.9 copy.30
  11.8 0.1 compare_and_fusion
  11.9 0.7 broadcast_multiply_fusion
  12.6 0.1 broadcast_select_fusion
  12.6 0.7 gather_fusion.1
  13.3 0.0 copy-done
  13.3 0.4 fusion.7
  13.8 3.0 %collective-permute-start = (bf16[2,128,128]{1,2,0:T(8,128)(2,1)S(1)}, bf16[2,128,128]{1,2,0:T(8,128)(2,1)S(1)}, u32[]{:S(2)}, u32[]{:S(2)}) collective-permute-start(bf16[2,128,128]{1,2,0:T(8,128)(2,1)S(1)} %fusion.7), channel_id=1, source_target_pairs={{24,0},{28,4},{0,8},{4,12},{8,16},{12,20},{16,24},{20,28},{25,1},{... | collective-permute-start | bytes 196616 | tf_op jit(solution)/shard_map/ppermute | solution.py:15
  16.8 0.0 collective-permute-start.1
  16.8 2.6 %collective-permute-start.2 = (bf16[2,128,128]{1,2,0:T(8,128)(2,1)S(1)}, bf16[2,128,128]{1,2,0:T(8,128)(2,1)S(1)}, u32[]{:S(2)}, u32[]{:S(2)}) collective-permute-start(bf16[2,128,128]{1,2,0:T(8,128)(2,1)S(1)} %fusion.7), channel_id=1, source_target_pairs={{4,0},{8,4},{12,8},{16,12},{20,16},{24,20},{28,24},{0,28},{5,1},{9... | collective-permute-start | bytes 196616 | tf_op jit(solution)/shard_map/ppermute | solution.py:15
  19.4 0.1 collective-permute-start.3
  19.5 0.1 eq.51
  19.6 0.3 collective-permute-done
  20.0 1.7 %collective-permute-done.1 = bf16[2,128,128]{1,2,0:T(8,128)(2,1)S(1)} collective-permute-done((bf16[2,128,128]{1,2,0:T(8,128)(2,1)S(1)}, bf16[2,128,128]{1,2,0:T(8,128)(2,1)S(1)}, u32[]{:S(2)}, u32[]{:S(2)}) %collective-permute-start.1) | collective-permute-done | bytes 65568 | tf_op jit(solution)/shard_map/ppermute | solution.py:15
  21.8 0.0 collective-permute-done.2
  21.8 1.9 %collective-permute-done.3 = bf16[2,128,128]{1,2,0:T(8,128)(2,1)S(1)} collective-permute-done((bf16[2,128,128]{1,2,0:T(8,128)(2,1)S(1)}, bf16[2,128,128]{1,2,0:T(8,128)(2,1)S(1)}, u32[]{:S(2)}, u32[]{:S(2)}) %collective-permute-start.3) | collective-permute-done | bytes 65568 | tf_op jit(solution)/shard_map/ppermute | solution.py:15
  23.7 0.7 gather_fusion.2
  24.4 0.9 convolution_bitcast_fusion
  25.3 1.6 %copy.33 = f32[2,12,128,128]{3,2,1,0:T(8,128)} copy(f32[2,12,128,128]{2,3,1,0:T(8,128)S(1)} %convolution_bitcast_fusion) | data formatting | bytes 3145728 | tf_op jit(solution)/shard_map/sik,snij->snkj/transpose | solution.py:60
  26.9 2.3 %copy.50 = f32[3,8,128,128]{3,1,2,0:T(8,128)S(1)} copy(f32[3,8,128,128]{3,2,1,0:T(8,128)} %bitcast.64) | data formatting | bytes 3145728
  29.3 0.3 copy.46
  29.5 2.2 %fusion = f32[2,5,2,128,128]{4,1,3,2,0:T(8,128)S(1)} fusion(f32[128,128,24,1,1]{1,0,2,4,3:T(8,128)S(1)} %bitcast.65, s32[2,5,2]{1,2,0:T(2,128)S(1)} %multiply_add_fusion, s32[24]{0:T(128)S(1)} %eq.51), kind=kOutput, calls=%fused_computation.4 | convolution fusion | flops 94372320 | bytes 2883760 | tf_op jit(solution)/shard_map/dot_general | solution.py:62
  31.8 0.0 copy-start.1
  31.8 2.1 %copy.35 = f32[2,5,2,128,128]{4,2,1,0,3:T(2,128)} copy(f32[2,5,2,128,128]{4,1,3,2,0:T(8,128)S(1)} %fusion) | data formatting | bytes 2621440 | tf_op jit(solution)/shard_map/dot_general | solution.py:62
  33.9 0.0 all-reduce.3.cloned.1.call-update
  33.9 0.0 copy-done.1
  33.9 0.6 dynamic-slice.5
  35.1 59.5 %all-reduce.3.cloned.1.call-done = f32[2,5,2,128,128]{4,2,1,0,3:T(2,128)} async-done(((f32[2,5,2,128,128]{4,2,1,0,3:T(2,128)}), f32[2,5,2,128,128]{4,2,1,0,3:T(2,128)}) %all-reduce.3.cloned.1.call-update) | async-done | bytes 1310736
  94.7 1.0 constant_dynamic-slice_fusion.5
  95.7 0.8 copy.36
  (11 shorter events, 0.1 us)
Async XLA Ops:
  6.5 6.8 %copy-start = (bf16[2,12,128,128]{3,2,1,0:T(8,128)(2,1)S(1)}, bf16[2,12,128,128]{3,2,1,0:T(8,128)(2,1)}, u32[]{:S(2)}) copy-start(bf16[2,12,128,128]{3,2,1,0:T(8,128)(2,1)} %param.6) | copy-start | bytes 2359300
  6.5 88.1 %all-reduce.3.cloned.1.call-start = ((), (), s32[]{:S(2)}) async-start(), calls=%async_computation | async-start | bytes 2621440
  13.8 6.2 %collective-permute-start = (bf16[2,128,128]{1,2,0:T(8,128)(2,1)S(1)}, bf16[2,128,128]{1,2,0:T(8,128)(2,1)S(1)}, u32[]{:S(2)}, u32[]{:S(2)}) collective-permute-start(bf16[2,128,128]{1,2,0:T(8,128)(2,1)S(1)} %fusion.7), channel_id=1, source_target_pairs={{24,0},{28,4},{0,8},{4,12},{8,16},{12,20},{16,24},{20,28},{25,1},{... | collective-permute-start | bytes 196616 | tf_op jit(solution)/shard_map/ppermute | solution.py:15
  16.8 5.0 %collective-permute-start.1 = (bf16[2,128,128]{1,2,0:T(8,128)(2,1)S(1)}, bf16[2,128,128]{1,2,0:T(8,128)(2,1)S(1)}, u32[]{:S(2)}, u32[]{:S(2)}) collective-permute-start(bf16[2,128,128]{1,2,0:T(8,128)(2,1)S(1)} %fusion.7), channel_id=1, source_target_pairs={{28,0},{0,4},{4,8},{8,12},{12,16},{16,20},{20,24},{24,28},{29,1},{... | collective-permute-start | bytes 196616 | tf_op jit(solution)/shard_map/ppermute | solution.py:15
  16.8 5.0 %collective-permute-start.2 = (bf16[2,128,128]{1,2,0:T(8,128)(2,1)S(1)}, bf16[2,128,128]{1,2,0:T(8,128)(2,1)S(1)}, u32[]{:S(2)}, u32[]{:S(2)}) collective-permute-start(bf16[2,128,128]{1,2,0:T(8,128)(2,1)S(1)} %fusion.7), channel_id=1, source_target_pairs={{4,0},{8,4},{12,8},{16,12},{20,16},{24,20},{28,24},{0,28},{5,1},{9... | collective-permute-start | bytes 196616 | tf_op jit(solution)/shard_map/ppermute | solution.py:15
  19.4 4.3 %collective-permute-start.3 = (bf16[2,128,128]{1,2,0:T(8,128)(2,1)S(1)}, bf16[2,128,128]{1,2,0:T(8,128)(2,1)S(1)}, u32[]{:S(2)}, u32[]{:S(2)}) collective-permute-start(bf16[2,128,128]{1,2,0:T(8,128)(2,1)S(1)} %fusion.7), channel_id=1, source_target_pairs={{8,0},{12,4},{16,8},{20,12},{24,16},{28,20},{0,24},{4,28},{9,1},{1... | collective-permute-start | bytes 196616 | tf_op jit(solution)/shard_map/ppermute | solution.py:15
  31.8 2.1 %copy-start.1 = (u32[32]{0:T(128)S(1)}, u32[32]{0:T(128)}, u32[]{:S(2)}) copy-start(u32[32]{0:T(128)} %constant.104) | copy-start | bytes 388
Sparse Core Ops, SparseCore 0:
  34.0 60.6 all-reduce.2
where the time goes:
time: 104 us; the launch traced here: 103 us
  waiting for transfers between devices  63.5 us (61%)
  between operations  14.8 us (14%)
  local copies, waits for them, and re-layouts  13.3 us (13%)
  starting transfers between devices  5.76 us (6%)
  matrix products  3.55 us (3%)
  other arithmetic  2.31 us (2%)
    unnamed x2, waiting for transfers between devices  59.5 us
    ppermute x4, starting transfers between devices, from_behind(): return lax.ppermute(block, axis, route)  5.76 us
    unnamed x13, local copies, waits for them, and re-layouts  5.2 us
    ppermute x4, waiting for transfers between devices, from_behind(): return lax.ppermute(block, axis, route)  3.99 us
    dot_general x1, matrix products, local(): jnp.dot(onehot, galerkin.reshape(-1, col_width * col_width), precision=la...  2.21 us
    dot_general x1, local copies, waits for them, and re-layouts, local(): jnp.dot(onehot, galerkin.reshape(-1, col_width * col_width), precision=la...  2.09 us
  transfers between devices with their start and end apart: 5, of which 4 were waited for; matrix products, arithmetic and copies ran while one was open for 1% of the time, Pallas kernels for 0%

commit v1 on v0

v1 whole, which is shorter than its diff:
```python
import functools

import jax
import jax.numpy as jnp
from jax import lax
from jax.experimental import pallas as pl
from jax.experimental.pallas import tpu as pltpu
from jax.sharding import PartitionSpec as P

NCG = 2
OFFSETS = 5
GROUP = 8
omega = 0.6

SMEM = pl.BlockSpec(memory_space=pltpu.SMEM)
VMEM = pl.BlockSpec(memory_space=pltpu.VMEM)


def from_behind(block, axis, distance):
    size = lax.axis_size(axis)
    return lax.ppermute(block, axis, [((i - distance) % size, i) for i in range(size)])


def from_sibling(block):
    size = lax.axis_size("blk")
    return lax.ppermute(block, "blk", [(i ^ 1, i) for i in range(size)])


def prolong_kernel(ids, neighbours, coarse_map, counts, blocks, tentative, inv_diag, out, pool):
    slots, nnz = neighbours.shape
    here = ids[0]
    live = counts[0]
    for slot in range(slots):
        pool[slot] = tentative[slot]
    pool[slots] = jnp.zeros_like(pool[slots])
    for row in range(slots):
        mine = coarse_map[here, 0, row]
        total = None
        for n in range(nnz):
            code = neighbours[row, n]
            slot = code - 2 * slots
            inside = (slot >= 0) & (slot < live)
            kept = inside & (coarse_map[here, 0, jnp.clip(slot, 0, slots - 1)] == mine)
            term = jnp.dot(
                blocks[row, n],
                pool[jnp.where(kept, slot, slots)],
                preferred_element_type=jnp.float32,
            )
            total = term if total is None else total + term
        width = out.shape[2]
        scale = jnp.broadcast_to(omega * inv_diag[row : row + 1, :], (width, inv_diag.shape[1])).T
        value = tentative[row].astype(jnp.float32) - scale * total
        out[row] = jnp.where(row < live, value, 0.0).astype(out.dtype)


def prolong_call(ids, neighbours, coarse_map, counts, blocks, tentative, inv_diag):
    slots, pores, width = tentative.shape
    return pl.pallas_call(
        prolong_kernel,
        out_shape=jax.ShapeDtypeStruct(tentative.shape, tentative.dtype),
        in_specs=[SMEM, SMEM, SMEM, SMEM, VMEM, VMEM, VMEM],
        out_specs=VMEM,
        scratch_shapes=[pltpu.VMEM((slots + 1, pores, width), tentative.dtype)],
        compiler_params=pltpu.CompilerParams(vmem_limit_bytes=16 << 20),
        cost_estimate=pl.CostEstimate(flops=100_000_000, bytes_accessed=1_000_000, transcendentals=0),
        name="prolong",
    )(ids, neighbours, coarse_map, counts, blocks, tentative, inv_diag)


def galerkin_kernel(places, parts, ids, neighbours, coarse_map, blocks, own, *refs):
    panels = len({p for parity in places for p in parity if p >= 0})
    extra = panels - (1 if 0 in places[0] and places[0][2] == 0 else 0)
    halo = refs[:extra]
    outs = refs[extra : extra + parts]
    pool, flipped, acc, todo = refs[extra + parts :]
    slots, nnz = neighbours.shape
    here, group = ids[0], ids[1]
    cycle = coarse_map.shape[0]
    odd = lax.rem(here, 2)

    first = panels - extra
    if first:
        for slot in range(slots):
            pool[slot] = own[slot]
    for i, panel in enumerate(halo):
        for slot in range(slots):
            pool[(first + i) * slots + slot] = panel[slot]
    for row in range(slots):
        flipped[row] = own[row].T
    dests = NCG * panels * NCG
    acc[...] = jnp.zeros_like(acc)

    for i in range(slots * nnz + GROUP):
        todo[i] = 0
        todo[i + slots * nnz + GROUP] = 0
        todo[i + 2 * (slots * nnz + GROUP)] = dests
    stride = slots * nnz + GROUP
    count = jnp.int32(0)
    for row in range(slots):
        mine = coarse_map[here, 0, row]
        for n in range(nnz):
            code = neighbours[row, n]
            offset = lax.div(code, slots)
            slot = code - offset * slots
            place = jnp.int32(-1)
            for o in range(OFFSETS):
                place = jnp.where(offset == o, jnp.where(odd == 1, places[1][o], places[0][o]), place)
            other = coarse_map[lax.rem(here + offset - 2 + cycle, cycle), 0, slot]
            wanted = place >= 0
            at = count
            todo[at] = row * nnz + n
            todo[at + stride] = jnp.where(wanted, place * slots + slot, 0)
            todo[at + 2 * stride] = jnp.where(wanted, (mine * panels + place) * NCG + other, dests)
            count = count + wanted.astype(jnp.int32)

    def some(step, carry):
        grams = []
        for j in range(GROUP):
            at = step * GROUP + j
            entry = todo[at]
            pair = jnp.dot(
                blocks[entry], pool[todo[at + stride]], preferred_element_type=jnp.float32
            ).astype(own.dtype)
            row = lax.div(entry, nnz)
            grams.append(jnp.dot(flipped[row], pair, preferred_element_type=jnp.float32))
        for j in range(GROUP):
            dest = todo[step * GROUP + j + 2 * stride]
            acc[dest] = acc[dest] + grams[j]
        return carry

    lax.fori_loop(0, lax.div(count + GROUP - 1, GROUP), some, 0)

    rows = outs[0].shape[1]
    for distance in range(parts):
        target = lax.rem(group + distance, parts)
        start = pl.multiple_of(target * rows, rows)
        for dest in range(dests):
            outs[distance][dest] = acc[dest, pl.ds(start, rows), :].astype(outs[distance].dtype)


def galerkin_call(places, parts, ids, neighbours, coarse_map, blocks, own, halo, name):
    slots, pores, width = own.shape
    nnz = neighbours.shape[1]
    panels = len({p for parity in places for p in parity if p >= 0})
    dests = NCG * panels * NCG
    rows = width // parts
    outs = [jax.ShapeDtypeStruct((dests, rows, width), jnp.float32 if d == 0 else own.dtype) for d in range(parts)]
    return pl.pallas_call(
        functools.partial(galerkin_kernel, places, parts),
        out_shape=outs,
        in_specs=[SMEM, SMEM, SMEM, VMEM, VMEM] + [VMEM] * len(halo),
        out_specs=[VMEM] * parts,
        scratch_shapes=[
            pltpu.VMEM((panels * slots, pores, width), own.dtype),
            pltpu.VMEM((slots, width, pores), own.dtype),
            pltpu.VMEM((dests + 1, width, width), jnp.float32),
            pltpu.SMEM((3 * (slots * nnz + GROUP),), jnp.int32),
        ],
        compiler_params=pltpu.CompilerParams(vmem_limit_bytes=24 << 20),
        cost_estimate=pl.CostEstimate(flops=200_000_000, bytes_accessed=2_000_000, transcendentals=0),
        name=name,
    )(ids, neighbours, coarse_map, blocks.reshape(slots * nnz, pores, pores), own, *halo)


NEAR = ((-1, -1, 0, 1, -1), (-1, 1, 0, -1, -1))
FAR = ((0, 2, -1, -1, 1), (0, -1, -1, 2, 1))


def finish_kernel(parts, ids, *refs):
    near, far, out = refs[:parts], refs[parts : 2 * parts], refs[2 * parts]
    odd = lax.rem(ids[0], 2) == 1
    for places, pieces in ((NEAR, near), (FAR, far)):
        panels = max(places[0]) + 1
        for c in range(NCG):
            for panel in range(panels):
                offset = jnp.where(odd, places[1].index(panel), places[0].index(panel))
                for c2 in range(NCG):
                    dest = (c * panels + panel) * NCG + c2
                    total = pieces[0][dest].astype(jnp.float32)
                    for piece in pieces[1:]:
                        total = total + piece[dest].astype(jnp.float32)
                    out[c, offset, c2] = total


def finish_call(ids, near, far, rows, width):
    parts = len(near)
    return pl.pallas_call(
        functools.partial(finish_kernel, parts),
        out_shape=jax.ShapeDtypeStruct((NCG, OFFSETS, NCG, rows, width), jnp.float32),
        in_specs=[SMEM] + [VMEM] * (2 * parts),
        out_specs=VMEM,
        compiler_params=pltpu.CompilerParams(vmem_limit_bytes=16 << 20),
        cost_estimate=pl.CostEstimate(flops=1_000_000, bytes_accessed=1_500_000, transcendentals=0),
        name="finish",
    )(ids, *near, *far)


def spread(pieces):
    parts = lax.axis_size("grp")
    rows = pieces[0].shape[1]
    return [pieces[0]] + [from_behind(pieces[d], "grp", d) for d in range(1, parts)]


def local(blocks, neighbours, tentative, inv_diag, coarse_map, counts):
    parts = lax.axis_size("grp")
    slots, pores, width = tentative.shape
    ids = jnp.stack([lax.axis_index("blk"), lax.axis_index("grp")]).astype(jnp.int32)
    own = prolong_call(ids, neighbours, coarse_map, counts, blocks, tentative, inv_diag)
    sibling = from_sibling(own)
    behind = from_behind(own, "blk", 2)
    ahead = from_behind(own, "blk", -2)
    odd = lax.rem(lax.axis_index("blk"), 2) == 1
    split = parts <= 4
    share = parts if split else 1
    near = galerkin_call(NEAR, share, ids, neighbours, coarse_map, blocks, own, [sibling], "near")
    if split:
        near = spread(near)
    other = from_sibling(jnp.where(odd, behind, ahead))
    far = galerkin_call(FAR, share, ids, neighbours, coarse_map, blocks, own, [behind, ahead, other], "far")
    if split:
        far = spread(far)
    else:
        near, far = [gathered(near[0], parts)], [gathered(far[0], parts)]
    return finish_call(ids, near, far, width // parts, width)


def gathered(whole, parts):
    dests, width, _ = whole.shape
    pieces = whole.astype(jnp.bfloat16).reshape(dests, parts, width // parts, width)
    arrived = lax.all_to_all(pieces, "grp", 1, 1, tiled=True)
    return jnp.sum(arrived.astype(jnp.float32), axis=1)


def solution(mesh):
    return jax.shard_map(
        local,
        mesh=mesh,
        in_specs=(
            P(("blk", "grp"), None, None, None),
            P(("blk", "grp"), None),
            P(("blk", "grp"), None, None),
            P(("blk", "grp"), None),
            P(None, "grp", None),
            P(("blk", "grp")),
        ),
        out_specs=P("blk", None, None, "grp", None),
        check_vma=False,
    )
```

time: 104 us -> 36.8 us (0.35)
  waiting for transfers between devices: 63.5 us -> 14.4 us
  between operations: 14.8 us -> 0.74 us
  local copies, waits for them, and re-layouts: 13.3 us -> 2.69 us
  starting transfers between devices: 5.76 us -> 12.9 us
  Pallas kernels: 0 us -> 6.05 us
  matrix products: 3.55 us -> 0 us
  other arithmetic: 2.31 us -> 0.08 us
    unnamed x2 -> x0, waiting for transfers between devices: 59.5 us -> none
    ppermute x4 -> x10, waiting for transfers between devices: 3.99 us -> 14.4 us  [the longest x8 14.3 us: from_behind(): lax.ppermute(block, axis, [((i - distance) % size, i) for i in range(size)])]
    ppermute x4 -> x10, starting transfers between devices: 5.76 us -> 12.9 us  [the longest x8 12.8 us: from_behind(): lax.ppermute(block, axis, [((i - distance) % size, i) for i in range(size)])]
    pallas_call x0 -> x4, Pallas kernels: none -> 6.05 us  [the longest x2 3.71 us: galerkin_call(): pl.pallas_call(functools.partial(galerkin_kernel, places, parts), out_sha...]
    dot_general x3 -> x0, matrix products: 3.55 us -> none  [the longest x1 2.21 us: local(): jnp.dot(onehot, galerkin.reshape(-1, col_width * col_width), precision=la...]
    unnamed x13, local copies, waits for them, and re-layouts: 5.2 us -> 2.69 us
    gather x4 -> x0, local copies, waits for them, and re-layouts: 2.17 us -> none  [the longest x2 0.78 us: local(): neighbour_map = window[neighbours]]
    dot_general x1 -> x0, local copies, waits for them, and re-layouts: 2.09 us -> none  [local(): jnp.dot(onehot, galerkin.reshape(-1, col_width * col_width), precision=la...]
  transfers between devices with their start and end apart: 5 -> 10, of which waited for: 4 -> 3; matrix products, arithmetic and copies ran while one was open for 1% -> 0% of each run, Pallas kernels for 0% -> 10%
where the time goes in v1:
time: 36.8 us
  waiting for transfers between devices  14.4 us (39%)
  starting transfers between devices  12.9 us (35%)
  Pallas kernels  6.05 us (16%)
  local copies, waits for them, and re-layouts  2.69 us (7%)
  between operations  0.74 us (2%)
    ppermute x8, waiting for transfers between devices, from_behind(): lax.ppermute(block, axis, [((i - distance) % size, i) for i in range(size)])  14.3 us
    ppermute x8, starting transfers between devices, from_behind(): lax.ppermute(block, axis, [((i - distance) % size, i) for i in range(size)])  12.8 us
    pallas_call x2, Pallas kernels, galerkin_call(): pl.pallas_call(functools.partial(galerkin_kernel, places, parts), out_sha...  3.71 us
    unnamed x13, local copies, waits for them, and re-layouts  2.69 us
    pallas_call x1, Pallas kernels, finish_call(): pl.pallas_call(functools.partial(finish_kernel, parts), out_shape=jax.Sha...  1.34 us
    pallas_call x1, Pallas kernels, prolong_call(): pl.pallas_call(prolong_kernel, out_shape=jax.ShapeDtypeStruct(tentative.s...  1 us
  transfers between devices with their start and end apart: 10, of which 3 were waited for; matrix products, arithmetic and copies ran while one was open for 0% of the time, Pallas kernels for 10%

profile of v1, /device:TPU:0, one launch (start us, length us, event | category | flops | bytes accessed | tf_op | source)
XLA Modules:
  0.0 36.8 jit_solution(15781673821110244706)
XLA Ops:
  0.0 0.0 copy-start.5
  0.7 0.0 copy-done.5
  0.7 0.1 copy.8.coarse_map
  0.8 0.0 copy-start.4
  0.8 0.0 copy-start.3
  0.8 0.1 pad_add_fusion.ids
  0.8 0.6 %copy-done.4 = f32[2,128]{1,0:T(2,128)S(1)} copy-done((f32[2,128]{1,0:T(2,128)S(1)}, f32[2,128]{1,0:T(2,128)}, u32[]{:S(2)}) %copy-start.4) | copy-done | bytes 1048
  1.4 0.0 copy-done.3
  1.5 0.0 copy-start
  1.5 1.1 %copy-done = bf16[2,12,128,128]{3,2,1,0:T(8,128)(2,1)S(1)} copy-done((bf16[2,12,128,128]{3,2,1,0:T(8,128)(2,1)S(1)}, bf16[2,12,128,128]{3,2,1,0:T(8,128)(2,1)}, u32[]{:S(2)}) %copy-start) | copy-done | bytes 786456
  2.6 0.0 copy-start.2
  2.6 0.8 %copy-done.2 = bf16[2,128,128]{2,1,0:T(8,128)(2,1)S(1)} copy-done((bf16[2,128,128]{2,1,0:T(8,128)(2,1)S(1)}, bf16[2,128,128]{2,1,0:T(8,128)(2,1)}, u32[]{:S(2)}) %copy-start.2) | copy-done | bytes 65560
  3.4 0.0 copy-start.1
  3.4 1.0 %prolong.1.own = bf16[2,128,128]{2,1,0:T(8,128)(2,1)S(1)} custom-call(s32[2]{0:T(128)S(1)} %pad_add_fusion.ids, s32[2,12]{1,0:T(2,128)S(1)} %copy-done.3, s32[8,1,2]{2,1,0:T(1,128)S(1)} %copy.8.coarse_map, s32[1]{0:T(128)S(6)} %copy.10.counts, bf16[2,12,128,128]{3,2,1,0:T(8,128)(2,1)S(1)} %copy-done, bf16[2,128,128]{2,1,0:T(8,128)(2,1)S(1)} %copy-done.2, ...), custom_call_target="tpu_custom_call" | custom-call | flops 100000000 | bytes 1000000 | tf_op jit(solution)/shard_map/prolong/pallas_call | solution.py:58
  4.4 3.9 %collective-permute-start.5 = (bf16[2,128,128]{2,1,0:T(8,128)(2,1)S(1)}, bf16[2,128,128]{2,1,0:T(8,128)(2,1)S(1)}, u32[]{:S(2)}, u32[]{:S(2)}) collective-permute-start(bf16[2,128,128]{2,1,0:T(8,128)(2,1)S(1)} %prolong.1.own), channel_id=1, source_target_pairs={{8,0},{12,4},{16,8},{20,12},{24,16},{28,20},{0,24},{4,28},{9,1},{1... | collective-permute-start | bytes 196616 | tf_op jit(solution)/shard_map/ppermute | solution.py:21
  8.4 0.0 collective-permute-start.4
  8.4 0.0 collective-permute-start
  8.4 2.1 %collective-permute-done.5.refs_1_ = bf16[2,128,128]{2,1,0:T(8,128)(2,1)S(1)} collective-permute-done((bf16[2,128,128]{2,1,0:T(8,128)(2,1)S(1)}, bf16[2,128,128]{2,1,0:T(8,128)(2,1)S(1)}, u32[]{:S(2)}, u32[]{:S(2)}) %collective-permute-start.5) | collective-permute-done | bytes 65568 | tf_op jit(solution)/shard_map/ppermute | solution.py:21
  10.4 3.1 %collective-permute-done.4.refs_0_ = bf16[2,128,128]{2,1,0:T(8,128)(2,1)S(1)} collective-permute-done((bf16[2,128,128]{2,1,0:T(8,128)(2,1)S(1)}, bf16[2,128,128]{2,1,0:T(8,128)(2,1)S(1)}, u32[]{:S(2)}, u32[]{:S(2)}) %collective-permute-start.4) | collective-permute-done | bytes 65568 | tf_op jit(solution)/shard_map/ppermute | solution.py:21
  13.6 0.1 collective-permute-start.6
  13.6 0.0 collective-permute-done.refs_0_
  13.6 0.0 copy-done.1
  13.7 1.8 %near.1 = (f32[8,32,128]{2,1,0:T(8,128)S(1)}, bf16[8,32,128]{2,1,0:T(8,128)(2,1)S(1)}, bf16[8,32,128]{2,1,0:T(8,128)(2,1)S(1)}, bf16[8,32,128]{2,1,0:T(8,128)(2,1)S(1)}) custom-call(s32[2]{0:T(128)S(1)} %pad_add_fusion.ids, s32[2,12]{1,0:T(2,128)S(1)} %copy-done.3, s32[8,1,2]{2,1,0:T(1,128)S(1)} %copy.8.coarse_map, bf16[24,128,128]{2,1,0:T(8,128)(2,1)S(1)} %bitcast.3, ...), custom_call_target="tpu_custom_call" | custom-call | flops 200000000 | bytes 2000000 | tf_op jit(solution)/shard_map/near/pallas_call | solution.py:148
  15.5 1.2 %collective-permute-start.1 = (bf16[8,32,128]{2,1,0:T(8,128)(2,1)S(1)}, bf16[8,32,128]{2,1,0:T(8,128)(2,1)S(1)}, u32[]{:S(2)}, u32[]{:S(2)}) collective-permute-start(bf16[8,32,128]{2,1,0:T(8,128)(2,1)S(1)} %get-tuple-element.14), channel_id=1, source_target_pairs={{3,0},{0,1},{1,2},{2,3},{7,4},{4,5},{5,6},{6,7},{11,8},{8,9},{9,10... | collective-permute-start | bytes 196616 | tf_op jit(solution)/shard_map/ppermute | solution.py:21
  16.8 0.0 collective-permute-done.6.refs_2_
  16.8 1.9 %far.1 = (f32[12,32,128]{2,1,0:T(8,128)S(1)}, bf16[12,32,128]{2,1,0:T(8,128)(2,1)S(1)}, bf16[12,32,128]{2,1,0:T(8,128)(2,1)S(1)}, bf16[12,32,128]{2,1,0:T(8,128)(2,1)S(1)}) custom-call(s32[2]{0:T(128)S(1)} %pad_add_fusion.ids, s32[2,12]{1,0:T(2,128)S(1)} %copy-done.3, s32[8,1,2]{2,1,0:T(1,128)S(1)} %copy.8.coarse_map, bf16[24,128,128]{2,1,0:T(8,128)(2,1)S(1)} %bitcast.4, ...), custom_call_target="tpu_custom_call" | custom-call | flops 200000000 | bytes 2000000 | tf_op jit(solution)/shard_map/far/pallas_call | solution.py:148
  18.6 2.0 %collective-permute-start.7 = (bf16[12,32,128]{2,1,0:T(8,128)(2,1)S(1)}, bf16[12,32,128]{2,1,0:T(8,128)(2,1)S(1)}, u32[]{:S(2)}, u32[]{:S(2)}) collective-permute-start(bf16[12,32,128]{2,1,0:T(8,128)(2,1)S(1)} %get-tuple-element.18), channel_id=1, source_target_pairs={{3,0},{0,1},{1,2},{2,3},{7,4},{4,5},{5,6},{6,7},{11,8},{8,9},{9,10... | collective-permute-start | bytes 294920 | tf_op jit(solution)/shard_map/ppermute | solution.py:21
  20.7 1.2 %collective-permute-start.8 = (bf16[12,32,128]{2,1,0:T(8,128)(2,1)S(1)}, bf16[12,32,128]{2,1,0:T(8,128)(2,1)S(1)}, u32[]{:S(2)}, u32[]{:S(2)}) collective-permute-start(bf16[12,32,128]{2,1,0:T(8,128)(2,1)S(1)} %get-tuple-element.19), channel_id=1, source_target_pairs={{2,0},{3,1},{0,2},{1,3},{6,4},{7,5},{4,6},{5,7},{10,8},{11,9},{8,1... | collective-permute-start | bytes 294920 | tf_op jit(solution)/shard_map/ppermute | solution.py:21
  21.9 2.3 %collective-permute-start.9 = (bf16[12,32,128]{2,1,0:T(8,128)(2,1)S(1)}, bf16[12,32,128]{2,1,0:T(8,128)(2,1)S(1)}, u32[]{:S(2)}, u32[]{:S(2)}) collective-permute-start(bf16[12,32,128]{2,1,0:T(8,128)(2,1)S(1)} %get-tuple-element.20), channel_id=1, source_target_pairs={{1,0},{2,1},{3,2},{0,3},{5,4},{6,5},{7,6},{4,7},{9,8},{10,9},{11,1... | collective-permute-start | bytes 294920 | tf_op jit(solution)/shard_map/ppermute | solution.py:21
  24.2 0.3 collective-permute-start.2
  24.5 0.0 collective-permute-done.1.refs_1_
  24.5 1.7 %collective-permute-start.3 = (bf16[8,32,128]{2,1,0:T(8,128)(2,1)S(1)}, bf16[8,32,128]{2,1,0:T(8,128)(2,1)S(1)}, u32[]{:S(2)}, u32[]{:S(2)}) collective-permute-start(bf16[8,32,128]{2,1,0:T(8,128)(2,1)S(1)} %get-tuple-element.16), channel_id=1, source_target_pairs={{1,0},{2,1},{3,2},{0,3},{5,4},{6,5},{7,6},{4,7},{9,8},{10,9},{11,1... | collective-permute-start | bytes 196616 | tf_op jit(solution)/shard_map/ppermute | solution.py:21
  26.3 9.2 %collective-permute-done.2.refs_2_ = bf16[8,32,128]{2,1,0:T(8,128)(2,1)S(1)} collective-permute-done((bf16[8,32,128]{2,1,0:T(8,128)(2,1)S(1)}, bf16[8,32,128]{2,1,0:T(8,128)(2,1)S(1)}, u32[]{:S(2)}, u32[]{:S(2)}) %collective-permute-start.2) | collective-permute-done | bytes 65568 | tf_op jit(solution)/shard_map/ppermute | solution.py:21
  35.5 0.0 collective-permute-done.3.refs_3_
  35.5 0.0 collective-permute-done.7.refs_5_
  35.5 0.0 collective-permute-done.8.refs_6_
  35.5 0.0 collective-permute-done.9.refs_7_
  35.5 1.3 %finish.1 = f32[2,5,2,32,128]{4,3,2,1,0:T(8,128)} custom-call(s32[2]{0:T(128)S(1)} %pad_add_fusion.ids, f32[8,32,128]{2,1,0:T(8,128)S(1)} %get-tuple-element.13.refs_0_, bf16[8,32,128]{2,1,0:T(8,128)(2,1)S(1)} %collective-permute-done.1.refs_1_, bf16[8,32,128]{2,1,0:T(8,128)(2,1)S(1)} %collective-permute-done.2.refs_2_, ...), custom_call_target="tpu_custom_call" | custom-call | flops 1000000 | bytes 1500000 | tf_op jit(solution)/shard_map/finish/pallas_call | solution.py:187
  (1 shorter events, 0.0 us)
Async XLA Ops:
  0.0 0.7 %copy-start.5 = (s32[8,1,2]{0,2,1:T(2,128)S(1)}, s32[8,1,2]{0,2,1:T(2,128)}, u32[]{:S(2)}) copy-start(s32[8,1,2]{0,2,1:T(2,128)} %param.10) | copy-start | bytes 196
  0.8 0.7 %copy-start.4 = (f32[2,128]{1,0:T(2,128)S(1)}, f32[2,128]{1,0:T(2,128)}, u32[]{:S(2)}) copy-start(f32[2,128]{1,0:T(2,128)} %inv_diag.1) | copy-start | bytes 3076
  0.8 0.7 %copy-start.3 = (s32[2,12]{1,0:T(2,128)S(1)}, s32[2,12]{1,0:T(2,128)}, u32[]{:S(2)}) copy-start(s32[2,12]{1,0:T(2,128)} %neighbours.5) | copy-start | bytes 292
  1.5 1.1 %copy-start = (bf16[2,12,128,128]{3,2,1,0:T(8,128)(2,1)S(1)}, bf16[2,12,128,128]{3,2,1,0:T(8,128)(2,1)}, u32[]{:S(2)}) copy-start(bf16[2,12,128,128]{3,2,1,0:T(8,128)(2,1)} %blocks.1) | copy-start | bytes 2359300
  2.6 0.8 %copy-start.2 = (bf16[2,128,128]{2,1,0:T(8,128)(2,1)S(1)}, bf16[2,128,128]{2,1,0:T(8,128)(2,1)}, u32[]{:S(2)}) copy-start(bf16[2,128,128]{2,1,0:T(8,128)(2,1)} %tentative.1) | copy-start | bytes 196612
  3.4 10.2 %copy-start.1 = (bf16[2,12,128,128]{3,2,1,0:T(8,128)(2,1)S(1)}, bf16[2,12,128,128]{3,2,1,0:T(8,128)(2,1)}, u32[]{:S(2)}) copy-start(bf16[2,12,128,128]{3,2,1,0:T(8,128)(2,1)} %blocks.1) | copy-start | bytes 2359300
  4.4 6.0 %collective-permute-start.5 = (bf16[2,128,128]{2,1,0:T(8,128)(2,1)S(1)}, bf16[2,128,128]{2,1,0:T(8,128)(2,1)S(1)}, u32[]{:S(2)}, u32[]{:S(2)}) collective-permute-start(bf16[2,128,128]{2,1,0:T(8,128)(2,1)S(1)} %prolong.1.own), channel_id=1, source_target_pairs={{8,0},{12,4},{16,8},{20,12},{24,16},{28,20},{0,24},{4,28},{9,1},{1... | collective-permute-start | bytes 196616 | tf_op jit(solution)/shard_map/ppermute | solution.py:21
  8.4 5.2 %collective-permute-start.4 = (bf16[2,128,128]{2,1,0:T(8,128)(2,1)S(1)}, bf16[2,128,128]{2,1,0:T(8,128)(2,1)S(1)}, u32[]{:S(2)}, u32[]{:S(2)}) collective-permute-start(bf16[2,128,128]{2,1,0:T(8,128)(2,1)S(1)} %prolong.1.own), channel_id=1, source_target_pairs={{24,0},{28,4},{0,8},{4,12},{8,16},{12,20},{16,24},{20,28},{25,1},{... | collective-permute-start | bytes 196616 | tf_op jit(solution)/shard_map/ppermute | solution.py:21
  8.4 5.3 %collective-permute-start = (bf16[2,128,128]{2,1,0:T(8,128)(2,1)S(1)}, bf16[2,128,128]{2,1,0:T(8,128)(2,1)S(1)}, u32[]{:S(2)}, u32[]{:S(2)}) collective-permute-start(bf16[2,128,128]{2,1,0:T(8,128)(2,1)S(1)} %prolong.1.own), channel_id=1, source_target_pairs={{4,0},{0,4},{12,8},{8,12},{20,16},{16,20},{28,24},{24,28},{5,1},{1... | collective-permute-start | bytes 196616 | tf_op jit(solution)/shard_map/ppermute | solution.py:26
  13.6 3.2 %collective-permute-start.6 = (bf16[2,128,128]{2,1,0:T(8,128)(2,1)S(1)}, bf16[2,128,128]{2,1,0:T(8,128)(2,1)S(1)}, u32[]{:S(2)}, u32[]{:S(2)}) collective-permute-start(bf16[2,128,128]{2,1,0:T(8,128)(2,1)S(1)} %broadcast_select_fusion), channel_id=1, source_target_pairs={{4,0},{0,4},{12,8},{8,12},{20,16},{16,20},{28,24},{24,28},{5,1},{1... | collective-permute-start | bytes 196616 | tf_op jit(solution)/shard_map/ppermute | solution.py:26
  15.5 9.0 %collective-permute-start.1 = (bf16[8,32,128]{2,1,0:T(8,128)(2,1)S(1)}, bf16[8,32,128]{2,1,0:T(8,128)(2,1)S(1)}, u32[]{:S(2)}, u32[]{:S(2)}) collective-permute-start(bf16[8,32,128]{2,1,0:T(8,128)(2,1)S(1)} %get-tuple-element.14), channel_id=1, source_target_pairs={{3,0},{0,1},{1,2},{2,3},{7,4},{4,5},{5,6},{6,7},{11,8},{8,9},{9,10... | collective-permute-start | bytes 196616 | tf_op jit(solution)/shard_map/ppermute | solution.py:21
  18.6 16.8 %collective-permute-start.7 = (bf16[12,32,128]{2,1,0:T(8,128)(2,1)S(1)}, bf16[12,32,128]{2,1,0:T(8,128)(2,1)S(1)}, u32[]{:S(2)}, u32[]{:S(2)}) collective-permute-start(bf16[12,32,128]{2,1,0:T(8,128)(2,1)S(1)} %get-tuple-element.18), channel_id=1, source_target_pairs={{3,0},{0,1},{1,2},{2,3},{7,4},{4,5},{5,6},{6,7},{11,8},{8,9},{9,10... | collective-permute-start | bytes 294920 | tf_op jit(solution)/shard_map/ppermute | solution.py:21
  20.7 14.8 %collective-permute-start.8 = (bf16[12,32,128]{2,1,0:T(8,128)(2,1)S(1)}, bf16[12,32,128]{2,1,0:T(8,128)(2,1)S(1)}, u32[]{:S(2)}, u32[]{:S(2)}) collective-permute-start(bf16[12,32,128]{2,1,0:T(8,128)(2,1)S(1)} %get-tuple-element.19), channel_id=1, source_target_pairs={{2,0},{3,1},{0,2},{1,3},{6,4},{7,5},{4,6},{5,7},{10,8},{11,9},{8,1... | collective-permute-start | bytes 294920 | tf_op jit(solution)/shard_map/ppermute | solution.py:21
  21.9 13.6 %collective-permute-start.9 = (bf16[12,32,128]{2,1,0:T(8,128)(2,1)S(1)}, bf16[12,32,128]{2,1,0:T(8,128)(2,1)S(1)}, u32[]{:S(2)}, u32[]{:S(2)}) collective-permute-start(bf16[12,32,128]{2,1,0:T(8,128)(2,1)S(1)} %get-tuple-element.20), channel_id=1, source_target_pairs={{1,0},{2,1},{3,2},{0,3},{5,4},{6,5},{7,6},{4,7},{9,8},{10,9},{11,1... | collective-permute-start | bytes 294920 | tf_op jit(solution)/shard_map/ppermute | solution.py:21
  24.2 11.3 %collective-permute-start.2 = (bf16[8,32,128]{2,1,0:T(8,128)(2,1)S(1)}, bf16[8,32,128]{2,1,0:T(8,128)(2,1)S(1)}, u32[]{:S(2)}, u32[]{:S(2)}) collective-permute-start(bf16[8,32,128]{2,1,0:T(8,128)(2,1)S(1)} %get-tuple-element.15), channel_id=1, source_target_pairs={{2,0},{3,1},{0,2},{1,3},{6,4},{7,5},{4,6},{5,7},{10,8},{11,9},{8,1... | collective-permute-start | bytes 196616 | tf_op jit(solution)/shard_map/ppermute | solution.py:21
  24.5 10.9 %collective-permute-start.3 = (bf16[8,32,128]{2,1,0:T(8,128)(2,1)S(1)}, bf16[8,32,128]{2,1,0:T(8,128)(2,1)S(1)}, u32[]{:S(2)}, u32[]{:S(2)}) collective-permute-start(bf16[8,32,128]{2,1,0:T(8,128)(2,1)S(1)} %get-tuple-element.16), channel_id=1, source_target_pairs={{1,0},{2,1},{3,2},{0,3},{5,4},{6,5},{7,6},{4,7},{9,8},{10,9},{11,1... | collective-permute-start | bytes 196616 | tf_op jit(solution)/shard_map/ppermute | solution.py:21

commit v2 on v0

v2 whole, which is shorter than its diff:
```python
import functools

import jax
import jax.numpy as jnp
from jax import lax
from jax.experimental import pallas as pl
from jax.experimental.pallas import tpu as pltpu
from jax.sharding import PartitionSpec as P

NCG = 2
OFFSETS = 5
NEAR = 2
FAR = 3
omega = 0.6

SMEM = pl.BlockSpec(memory_space=pltpu.SMEM)
VMEM = pl.BlockSpec(memory_space=pltpu.VMEM)
ANY = pl.BlockSpec(memory_space=pltpu.HBM)


def from_behind(block, axis, distance):
    size = lax.axis_size(axis)
    return lax.ppermute(block, axis, [((i - distance) % size, i) for i in range(size)])


def from_sibling(block):
    size = lax.axis_size("blk")
    return lax.ppermute(block, "blk", [(i ^ 1, i) for i in range(size)])


def from_across(block):
    size = lax.axis_size("blk")
    return lax.ppermute(block, "blk", [((i + (1 if i % 2 else -1)) % size, i) for i in range(size)])


def prolong_kernel(counts, neighbours, coarse_map, blocks, tentative, inv_diag, out, flipped, todo,
                   held, base, scale, codes, groups, table, sems):
    slots, nnz = neighbours.shape
    cycle = coarse_map.shape[2]
    small = [
        pltpu.make_async_copy(source, target, sems.at[i])
        for i, (source, target) in enumerate(((neighbours, codes), (coarse_map, groups)))
    ]
    large = [
        pltpu.make_async_copy(tentative, base.at[pl.ds(0, slots)], sems.at[2]),
        pltpu.make_async_copy(inv_diag, scale, sems.at[3]),
    ] + [pltpu.make_async_copy(blocks.at[row], held.at[row], sems.at[4 + row]) for row in range(slots)]
    for copy in small + large:
        copy.start()
    base[slots] = jnp.zeros_like(base[slots])

    here = lax.axis_index("blk")
    odd = lax.rem(here, 2)
    beside = 3 - 2 * odd
    for copy in small:
        copy.wait()
    live = counts[0]
    mine = [groups[0, row, here] for row in range(slots)]
    for offset in range(OFFSETS):
        there = here + (offset - 2)
        there = jnp.where(there < 0, there + cycle, jnp.where(there >= cycle, there - cycle, there))
        if offset in (1, 3):
            first = beside == offset
            panel = jnp.where(first, 1, 2)
            stride = jnp.where(first, NEAR * NCG, FAR * NCG)
        else:
            first = jnp.bool_(offset == 2)
            panel = {2: 0, 0: 0, 4: 1}[offset]
            stride = (NEAR if offset == 2 else FAR) * NCG
        for slot in range(slots):
            other = groups[0, slot, there]
            for row in range(slots):
                at = row * OFFSETS * slots + offset * slots + slot
                word = 256 * (panel * slots + slot) + 65536 * (mine[row] * stride + panel * NCG + other)
                table[at] = word + jnp.where(first, 1 << 30, 0)
    keep = [[jnp.where((mine[slot] == mine[row]) & (slot < live), slot, slots) for slot in range(slots)]
            for row in range(slots)]
    near = jnp.int32(0)
    kept = []
    for row in range(slots):
        for n in range(nnz):
            entry = row * nnz + n
            code = codes[row, n]
            chosen = jnp.int32(slots)
            for slot in range(slots):
                chosen = jnp.where(code == 2 * slots + slot, keep[row][slot], chosen)
            kept.append(chosen)
            word = table[row * OFFSETS * slots + code]
            first = lax.shift_right_logical(word, 30)
            at = jnp.where(first == 1, near, slots * nnz - 1 - entry + near)
            todo[at] = (word & ((1 << 30) - 1)) + entry
            near = near + first
    todo[slots * nnz] = near
    todo[slots * nnz + 1] = odd
    todo[slots * nnz + 2] = lax.axis_index("grp")

    for copy in large[:2]:
        copy.wait()
    width = out.shape[2]
    for row in range(slots):
        large[2 + row].wait()
        total = None
        for n in range(nnz):
            term = jnp.dot(held[row, n], base[kept[row * nnz + n]], preferred_element_type=jnp.float32)
            total = term if total is None else total + term
        factor = jnp.broadcast_to(omega * scale[row : row + 1, :], (width, scale.shape[1])).T
        value = base[row].astype(jnp.float32) - factor * total
        value = jnp.where(row < live, value, 0.0).astype(out.dtype)
        out[row] = value
        flipped[row] = value.T


def prolong_call(counts, *arrays):
    neighbours, coarse_map, blocks, tentative, inv_diag = arrays
    slots, pores, width = tentative.shape
    nnz = neighbours.shape[1]
    arrays = [pltpu.with_memory_space_constraint(x, pltpu.HBM) for x in arrays]
    return pl.pallas_call(
        prolong_kernel,
        out_shape=(
            jax.ShapeDtypeStruct(tentative.shape, tentative.dtype),
            jax.ShapeDtypeStruct((slots, width, pores), tentative.dtype),
            jax.ShapeDtypeStruct((slots * nnz + 8,), jnp.int32),
        ),
        in_specs=[SMEM] + [ANY] * len(arrays),
        out_specs=(VMEM, VMEM, SMEM),
        scratch_shapes=[
            pltpu.VMEM(blocks.shape, blocks.dtype),
            pltpu.VMEM((slots + 1, pores, width), tentative.dtype),
            pltpu.VMEM(inv_diag.shape, inv_diag.dtype),
            pltpu.SMEM(neighbours.shape, jnp.int32),
            pltpu.SMEM(coarse_map.shape, jnp.int32),
            pltpu.SMEM((slots * OFFSETS * slots,), jnp.int32),
            pltpu.SemaphoreType.DMA((4 + slots,)),
        ],
        compiler_params=pltpu.CompilerParams(vmem_limit_bytes=16 << 20),
        cost_estimate=pl.CostEstimate(flops=100_000_000, bytes_accessed=1_000_000, transcendentals=0),
        name="prolong",
    )(counts, *arrays)


def galerkin_kernel(far, layout, parts, nnz, todo, blocks, flipped, *refs):
    slots = flipped.shape[0]
    panels = FAR if far else NEAR
    dests = NCG * panels * NCG
    halo, refs = refs[:panels], refs[panels:]
    carried, refs = refs[: sum(carry for _, carry in layout)], refs[sum(carry for _, carry in layout) :]
    outs, (pool, acc) = refs[: len(layout)], refs[len(layout) :]
    for panel in range(panels):
        for slot in range(slots):
            pool[panel * slots + slot] = halo[panel][slot]
    acc[...] = jnp.zeros_like(acc)
    entries = slots * nnz
    near = todo[entries]
    count = entries - near if far else near

    def some(step, carry):
        grams, places = [], []
        for j in range(nnz):
            at = step * nnz + j
            word = todo[entries - 1 - at if far else at]
            dest = lax.shift_right_logical(word, 16)
            panel = lax.shift_right_logical(word, 8) & 255
            entry = word & 255
            inside = at < count
            places.append(jnp.where(inside, dest, dests))
            panel = jnp.where(inside, panel, 0)
            row = lax.div(entry, nnz)
            pair = jnp.dot(blocks[entry], pool[panel], preferred_element_type=jnp.float32).astype(pool.dtype)
            grams.append(jnp.dot(flipped[row], pair, preferred_element_type=jnp.float32))
        for place, gram in zip(places, grams):
            acc[place] = acc[place] + gram
        return carry

    lax.fori_loop(0, lax.div(count + nnz - 1, nnz), some, 0)

    for (distance, carry), out in zip(layout, outs):
        rows = out.shape[1]
        start = 0
        if parts > 1:
            target = lax.rem(todo[entries + 2] + distance, parts)
            start = pl.multiple_of(target * rows, rows)
        skip = out.shape[0] - dests
        if carry:
            source, carried = carried[0], carried[1:]
            out[pl.ds(0, skip)] = source[...]
        for dest in range(dests):
            out[skip + dest] = acc[dest, pl.ds(start, rows), :].astype(out.dtype)


def galerkin_call(far, layout, parts, todo, blocks, flipped, halo, carried):
    slots, width, pores = flipped.shape
    nnz = blocks.shape[1]
    panels = FAR if far else NEAR
    dests = NCG * panels * NCG
    rows = width // parts
    before = [carried[0].shape[0] if carry else 0 for _, carry in layout]
    return pl.pallas_call(
        functools.partial(galerkin_kernel, far, layout, parts, nnz),
        out_shape=[
            jax.ShapeDtypeStruct((skip + dests, rows, width), flipped.dtype if distance else jnp.float32)
            for (distance, _), skip in zip(layout, before)
        ],
        in_specs=[SMEM, VMEM, VMEM] + [VMEM] * (len(halo) + len(carried)),
        out_specs=[VMEM] * len(layout),
        scratch_shapes=[
            pltpu.VMEM((panels * slots, pores, width), flipped.dtype),
            pltpu.VMEM((dests + 1, width, width), jnp.float32),
        ],
        compiler_params=pltpu.CompilerParams(vmem_limit_bytes=24 << 20),
        cost_estimate=pl.CostEstimate(flops=200_000_000, bytes_accessed=2_000_000, transcendentals=0),
        name="far" if far else "near",
    )(todo, blocks.reshape(slots * nnz, pores, pores), flipped, *halo, *carried)


def finish_kernel(at_odd, nears, fars, boths, todo, *refs):
    near, refs = refs[:nears], refs[nears:]
    far, refs = refs[:fars], refs[fars:]
    both, out = refs[:boths], refs[boths]
    odd = todo[at_odd] == 1
    skip = NCG * NEAR * NCG
    for pieces, panels, first in ((near, NEAR, 0), (far, FAR, skip)):
        for c in range(NCG):
            for panel in range(panels):
                if panels == NEAR:
                    offset = jnp.where(odd, 1, 3) if panel else 2
                else:
                    offset = (0, 4, jnp.where(odd, 3, 1))[panel]
                for c2 in range(NCG):
                    dest = (c * panels + panel) * NCG + c2
                    total = pieces[0][dest].astype(jnp.float32)
                    for piece in pieces[1:]:
                        total = total + piece[dest].astype(jnp.float32)
                    for piece in both:
                        total = total + piece[first + dest].astype(jnp.float32)
                    out[c, offset, c2] = total


def finish_call(at_odd, todo, near, far, both, rows, width):
    return pl.pallas_call(
        functools.partial(finish_kernel, at_odd, len(near), len(far), len(both)),
        out_shape=jax.ShapeDtypeStruct((NCG, OFFSETS, NCG, rows, width), jnp.float32),
        in_specs=[SMEM] + [VMEM] * (len(near) + len(far) + len(both)),
        out_specs=VMEM,
        compiler_params=pltpu.CompilerParams(vmem_limit_bytes=16 << 20),
        cost_estimate=pl.CostEstimate(flops=1_000_000, bytes_accessed=1_500_000, transcendentals=0),
        name="finish",
    )(todo, *near, *far, *both)


def local(blocks, neighbours, tentative, inv_diag, coarse_map, counts):
    parts = lax.axis_size("grp")
    slots, pores, width = tentative.shape
    nnz = neighbours.shape[1]
    own, flipped, todo = prolong_call(
        counts, neighbours, jnp.transpose(coarse_map, (1, 2, 0)), blocks, tentative, inv_diag
    )
    sibling = from_sibling(own)
    behind = from_behind(own, "blk", 2)
    ahead = from_behind(own, "blk", -2)
    across = from_across(own)

    split = parts <= 4
    share = parts if split else 1
    early = EARLY[parts] if split else []
    late = LATE[parts] if split else []
    layout = [(0, False)] + [(d, False) for d in early + late]
    near = galerkin_call(False, layout, share, todo, blocks, flipped, [own, sibling], [])
    near_own, near_early, near_late = near[0], near[1 : 1 + len(early)], near[1 + len(early) :]
    near_early = [from_behind(piece, "grp", d) for piece, d in zip(near_early, early)]
    layout = [(0, False)] + [(d, False) for d in early] + [(d, True) for d in late]
    far = galerkin_call(True, layout, share, todo, blocks, flipped, [behind, ahead, across], near_late)
    if GATE:
        near_early, far = lax.optimization_barrier((near_early, far))
    far_own, far_early, both = far[0], far[1 : 1 + len(early)], far[1 + len(early) :]
    order = [d for d in ORDER[parts]] if split else []
    moved = {d: from_behind(piece, "grp", d) for d, piece in sorted(
        zip(early + late, far_early + both), key=lambda item: order.index(item[0]))}
    far_early = [moved[d] for d in early]
    both = [moved[d] for d in late]
    if not split:
        near_own, far_own = gathered(near_own, parts), gathered(far_own, parts)
    return finish_call(
        slots * nnz + 1, todo, [near_own] + near_early, [far_own] + far_early, both, width // parts, width
    )


GATE = True
EARLY = {1: [], 2: [1], 3: [1], 4: [1, 3]}
LATE = {1: [], 2: [], 3: [2], 4: [2]}
ORDER = {1: [], 2: [1], 3: [1, 2], 4: [2, 1, 3]}


def gathered(whole, parts):
    dests, width, _ = whole.shape
    pieces = whole.astype(jnp.bfloat16).reshape(dests, parts, width // parts, width)
    arrived = lax.all_to_all(pieces, "grp", 1, 1, tiled=True)
    return jnp.sum(arrived.astype(jnp.float32), axis=1)


def solution(mesh):
    return jax.shard_map(
        local,
        mesh=mesh,
        in_specs=(
            P(("blk", "grp"), None, None, None),
            P(("blk", "grp"), None),
            P(("blk", "grp"), None, None),
            P(("blk", "grp"), None),
            P(None, "grp", None),
            P(("blk", "grp")),
        ),
        out_specs=P("blk", None, None, "grp", None),
        check_vma=False,
    )
```

time: 104 us -> 29.9 us (0.29)
  the two profiles are of different devices: /device:TPU:0 before, /device:TPU:10 now
where the time goes in v2:
time: 29.9 us; the launch traced here: 30.1 us
  waiting for transfers between devices  13.2 us (44%)
  starting transfers between devices  9.94 us (33%)
  Pallas kernels  6.16 us (21%)
  between operations  0.77 us (3%)
    ppermute x7, waiting for transfers between devices, from_behind(): lax.ppermute(block, axis, [((i - distance) % size, i) for i in range(size)])  13.2 us
    ppermute x7, starting transfers between devices, from_behind(): lax.ppermute(block, axis, [((i - distance) % size, i) for i in range(size)])  9.23 us
    pallas_call x2, Pallas kernels, galerkin_call(): pl.pallas_call(functools.partial(galerkin_kernel, far, layout, parts, nnz...  2.71 us
    pallas_call x1, Pallas kernels, prolong_call(): pl.pallas_call(prolong_kernel, out_shape=(jax.ShapeDtypeStruct(tentative....  2.12 us
    pallas_call x1, Pallas kernels, finish_call(): pl.pallas_call(functools.partial(finish_kernel, at_odd, len(near), len(fa...  1.33 us
    ppermute x1, starting transfers between devices, from_across(): lax.ppermute(block, 'blk', [((i + (1 if i % 2 else -1)) % size, i) for i...  0.64 us
  transfers between devices with their start and end apart: 9, of which 5 were waited for; matrix products, arithmetic and copies ran while one was open for 0% of the time, Pallas kernels for 9%

profile of v2, /device:TPU:10, one launch (start us, length us, event | category | flops | bytes accessed | tf_op | source)
XLA Modules:
  0.0 30.1 jit_solution(10101280092404863321)
XLA Ops:
  0.0 0.0 copy-start
  0.7 2.1 %prolong.1 = (bf16[2,128,128]{2,1,0:T(8,128)(2,1)S(1)}, bf16[2,128,128]{2,1,0:T(8,128)(2,1)S(1)}, s32[32]{0:T(128)S(1)}) custom-call(s32[1]{0:T(128)S(6)} %copy.7.counts, s32[2,12]{1,0:T(2,128)} %neighbours.1, s32[1,2,8]{2,1,0:T(2,128)} %bitcast.4, bf16[2,12,128,128]{3,2,1,0:T(8,128)(2,1)} %blocks.1, bf16[2,128,128]{2,1,0:T(8,128)(2,1)} %tentative.1, ...), custom_call_target="tpu_custom_call" | custom-call | flops 100000000 | bytes 1000000 | tf_op jit(solution)/shard_map/prolong/pallas_call | solution.py:118
  2.9 0.1 collective-permute-start
  2.9 0.6 %collective-permute-start.5 = (bf16[2,128,128]{2,1,0:T(8,128)(2,1)S(1)}, bf16[2,128,128]{2,1,0:T(8,128)(2,1)S(1)}, u32[]{:S(2)}, u32[]{:S(2)}) collective-permute-start(bf16[2,128,128]{2,1,0:T(8,128)(2,1)S(1)} %get-tuple-element.24.refs_0_), channel_id=1, source_target_pairs={{28,0},{8,4},{4,8},{16,12},{12,16},{24,20},{20,24},{0,28},{29,1},{... | collective-permute-start | bytes 196616 | tf_op jit(solution)/shard_map/ppermute | solution.py:33
  3.6 2.4 %collective-permute-start.4 = (bf16[2,128,128]{2,1,0:T(8,128)(2,1)S(1)}, bf16[2,128,128]{2,1,0:T(8,128)(2,1)S(1)}, u32[]{:S(2)}, u32[]{:S(2)}) collective-permute-start(bf16[2,128,128]{2,1,0:T(8,128)(2,1)S(1)} %get-tuple-element.24.refs_0_), channel_id=1, source_target_pairs={{8,0},{12,4},{16,8},{20,12},{24,16},{28,20},{0,24},{4,28},{9,1},{1... | collective-permute-start | bytes 196616 | tf_op jit(solution)/shard_map/ppermute | solution.py:23
  6.0 0.5 %collective-permute-start.3 = (bf16[2,128,128]{2,1,0:T(8,128)(2,1)S(1)}, bf16[2,128,128]{2,1,0:T(8,128)(2,1)S(1)}, u32[]{:S(2)}, u32[]{:S(2)}) collective-permute-start(bf16[2,128,128]{2,1,0:T(8,128)(2,1)S(1)} %get-tuple-element.24.refs_0_), channel_id=1, source_target_pairs={{24,0},{28,4},{0,8},{4,12},{8,16},{12,20},{16,24},{20,28},{25,1},{... | collective-permute-start | bytes 196616 | tf_op jit(solution)/shard_map/ppermute | solution.py:23
  6.5 0.0 collective-permute-done.refs_1_
  6.5 0.0 copy-done
  6.5 1.1 %near.1 = (f32[8,32,128]{2,1,0:T(8,128)S(1)}, bf16[8,32,128]{2,1,0:T(8,128)(2,1)S(1)}, bf16[8,32,128]{2,1,0:T(8,128)(2,1)S(1)}, bf16[8,32,128]{2,1,0:T(8,128)(2,1)S(1)}) custom-call(s32[32]{0:T(128)S(1)} %get-tuple-element.22.todo, bf16[24,128,128]{2,1,0:T(8,128)(2,1)S(1)} %bitcast.2, bf16[2,128,128]{2,1,0:T(8,128)(2,1)S(1)} %get-tuple-element.23.flipped, ...), custom_call_target="tpu_custom_call" | custom-call | flops 200000000 | bytes 2000000 | tf_op jit(solution)/shard_map/near/pallas_call | solution.py:198
  7.6 1.6 %collective-permute-start.1 = (bf16[8,32,128]{2,1,0:T(8,128)(2,1)S(1)}, bf16[8,32,128]{2,1,0:T(8,128)(2,1)S(1)}, u32[]{:S(2)}, u32[]{:S(2)}) collective-permute-start(bf16[8,32,128]{2,1,0:T(8,128)(2,1)S(1)} %get-tuple-element.26), channel_id=1, source_target_pairs={{3,0},{0,1},{1,2},{2,3},{7,4},{4,5},{5,6},{6,7},{11,8},{8,9},{9,10... | collective-permute-start | bytes 196616 | tf_op jit(solution)/shard_map/ppermute | solution.py:23
  9.2 0.4 %collective-permute-start.2 = (bf16[8,32,128]{2,1,0:T(8,128)(2,1)S(1)}, bf16[8,32,128]{2,1,0:T(8,128)(2,1)S(1)}, u32[]{:S(2)}, u32[]{:S(2)}) collective-permute-start(bf16[8,32,128]{2,1,0:T(8,128)(2,1)S(1)} %get-tuple-element.27), channel_id=1, source_target_pairs={{1,0},{2,1},{3,2},{0,3},{5,4},{6,5},{7,6},{4,7},{9,8},{10,9},{11,1... | collective-permute-start | bytes 196616 | tf_op jit(solution)/shard_map/ppermute | solution.py:23
  9.7 0.0 collective-permute-done.5.refs_2_
  9.7 0.4 %collective-permute-done.4.refs_1_ = bf16[2,128,128]{2,1,0:T(8,128)(2,1)S(1)} collective-permute-done((bf16[2,128,128]{2,1,0:T(8,128)(2,1)S(1)}, bf16[2,128,128]{2,1,0:T(8,128)(2,1)S(1)}, u32[]{:S(2)}, u32[]{:S(2)}) %collective-permute-start.4) | collective-permute-done | bytes 65568 | tf_op jit(solution)/shard_map/ppermute | solution.py:23
  10.1 0.6 %collective-permute-done.3.refs_0_ = bf16[2,128,128]{2,1,0:T(8,128)(2,1)S(1)} collective-permute-done((bf16[2,128,128]{2,1,0:T(8,128)(2,1)S(1)}, bf16[2,128,128]{2,1,0:T(8,128)(2,1)S(1)}, u32[]{:S(2)}, u32[]{:S(2)}) %collective-permute-start.3) | collective-permute-done | bytes 65568 | tf_op jit(solution)/shard_map/ppermute | solution.py:23
  10.7 1.6 %far.1 = (f32[12,32,128]{2,1,0:T(8,128)S(1)}, bf16[12,32,128]{2,1,0:T(8,128)(2,1)S(1)}, bf16[12,32,128]{2,1,0:T(8,128)(2,1)S(1)}, bf16[20,32,128]{2,1,0:T(8,128)(2,1)S(1)}) custom-call(s32[32]{0:T(128)S(1)} %get-tuple-element.22.todo, bf16[24,128,128]{2,1,0:T(8,128)(2,1)S(1)} %bitcast.3, bf16[2,128,128]{2,1,0:T(8,128)(2,1)S(1)} %get-tuple-element.23.flipped, ...), custom_call_target="tpu_custom_call" | custom-call | flops 200000000 | bytes 2000000 | tf_op jit(solution)/shard_map/far/pallas_call | solution.py:198
  12.3 0.0 collective-permute-done.1.refs_1_
  12.3 2.1 %collective-permute-done.2.refs_2_ = bf16[8,32,128]{2,1,0:T(8,128)(2,1)S(1)} collective-permute-done((bf16[8,32,128]{2,1,0:T(8,128)(2,1)S(1)}, bf16[8,32,128]{2,1,0:T(8,128)(2,1)S(1)}, u32[]{:S(2)}, u32[]{:S(2)}) %collective-permute-start.2) | collective-permute-done | bytes 65568 | tf_op jit(solution)/shard_map/ppermute | solution.py:23
  14.4 2.2 %collective-permute-start.8 = (bf16[20,32,128]{2,1,0:T(8,128)(2,1)S(1)}, bf16[20,32,128]{2,1,0:T(8,128)(2,1)S(1)}, u32[]{:S(2)}, u32[]{:S(2)}) collective-permute-start(bf16[20,32,128]{2,1,0:T(8,128)(2,1)S(1)} %get-tuple-element.38), channel_id=1, source_target_pairs={{2,0},{3,1},{0,2},{1,3},{6,4},{7,5},{4,6},{5,7},{10,8},{11,9},{8,1... | collective-permute-start | bytes 491528 | tf_op jit(solution)/shard_map/ppermute | solution.py:23
  16.6 0.5 %collective-permute-start.6 = (bf16[12,32,128]{2,1,0:T(8,128)(2,1)S(1)}, bf16[12,32,128]{2,1,0:T(8,128)(2,1)S(1)}, u32[]{:S(2)}, u32[]{:S(2)}) collective-permute-start(bf16[12,32,128]{2,1,0:T(8,128)(2,1)S(1)} %get-tuple-element.36), channel_id=1, source_target_pairs={{3,0},{0,1},{1,2},{2,3},{7,4},{4,5},{5,6},{6,7},{11,8},{8,9},{9,10... | collective-permute-start | bytes 294920 | tf_op jit(solution)/shard_map/ppermute | solution.py:23
  17.1 1.6 %collective-permute-start.7 = (bf16[12,32,128]{2,1,0:T(8,128)(2,1)S(1)}, bf16[12,32,128]{2,1,0:T(8,128)(2,1)S(1)}, u32[]{:S(2)}, u32[]{:S(2)}) collective-permute-start(bf16[12,32,128]{2,1,0:T(8,128)(2,1)S(1)} %get-tuple-element.37), channel_id=1, source_target_pairs={{1,0},{2,1},{3,2},{0,3},{5,4},{6,5},{7,6},{4,7},{9,8},{10,9},{11,1... | collective-permute-start | bytes 294920 | tf_op jit(solution)/shard_map/ppermute | solution.py:23
  18.6 7.9 %collective-permute-done.6.refs_4_ = bf16[12,32,128]{2,1,0:T(8,128)(2,1)S(1)} collective-permute-done((bf16[12,32,128]{2,1,0:T(8,128)(2,1)S(1)}, bf16[12,32,128]{2,1,0:T(8,128)(2,1)S(1)}, u32[]{:S(2)}, u32[]{:S(2)}) %collective-permute-start.6) | collective-permute-done | bytes 98336 | tf_op jit(solution)/shard_map/ppermute | solution.py:23
  26.6 2.2 %collective-permute-done.7.refs_5_ = bf16[12,32,128]{2,1,0:T(8,128)(2,1)S(1)} collective-permute-done((bf16[12,32,128]{2,1,0:T(8,128)(2,1)S(1)}, bf16[12,32,128]{2,1,0:T(8,128)(2,1)S(1)}, u32[]{:S(2)}, u32[]{:S(2)}) %collective-permute-start.7) | collective-permute-done | bytes 98336 | tf_op jit(solution)/shard_map/ppermute | solution.py:23
  28.7 0.0 collective-permute-done.8.refs_6_
  28.7 1.3 %finish.1 = f32[2,5,2,32,128]{4,3,2,1,0:T(8,128)} custom-call(s32[32]{0:T(128)S(1)} %get-tuple-element.22.todo, f32[8,32,128]{2,1,0:T(8,128)S(1)} %get-tuple-element.25.refs_0_, bf16[8,32,128]{2,1,0:T(8,128)(2,1)S(1)} %collective-permute-done.1.refs_1_, bf16[8,32,128]{2,1,0:T(8,128)(2,1)S(1)} %collective-permute-done.2.refs_2_, ...), custom_call_target="tpu_custom_call" | custom-call | flops 1000000 | bytes 1500000 | tf_op jit(solution)/shard_map/finish/pallas_call | solution.py:240
Async XLA Ops:
  0.0 6.5 %copy-start = (bf16[2,12,128,128]{3,2,1,0:T(8,128)(2,1)S(1)}, bf16[2,12,128,128]{3,2,1,0:T(8,128)(2,1)}, u32[]{:S(2)}) copy-start(bf16[2,12,128,128]{3,2,1,0:T(8,128)(2,1)} %blocks.1) | copy-start | bytes 2359300
  2.9 3.6 %collective-permute-start = (bf16[2,128,128]{2,1,0:T(8,128)(2,1)S(1)}, bf16[2,128,128]{2,1,0:T(8,128)(2,1)S(1)}, u32[]{:S(2)}, u32[]{:S(2)}) collective-permute-start(bf16[2,128,128]{2,1,0:T(8,128)(2,1)S(1)} %get-tuple-element.24.refs_0_), channel_id=1, source_target_pairs={{4,0},{0,4},{12,8},{8,12},{20,16},{16,20},{28,24},{24,28},{5,1},{1... | collective-permute-start | bytes 196616 | tf_op jit(solution)/shard_map/ppermute | solution.py:28
  2.9 6.8 %collective-permute-start.5 = (bf16[2,128,128]{2,1,0:T(8,128)(2,1)S(1)}, bf16[2,128,128]{2,1,0:T(8,128)(2,1)S(1)}, u32[]{:S(2)}, u32[]{:S(2)}) collective-permute-start(bf16[2,128,128]{2,1,0:T(8,128)(2,1)S(1)} %get-tuple-element.24.refs_0_), channel_id=1, source_target_pairs={{28,0},{8,4},{4,8},{16,12},{12,16},{24,20},{20,24},{0,28},{29,1},{... | collective-permute-start | bytes 196616 | tf_op jit(solution)/shard_map/ppermute | solution.py:33
  3.6 6.5 %collective-permute-start.4 = (bf16[2,128,128]{2,1,0:T(8,128)(2,1)S(1)}, bf16[2,128,128]{2,1,0:T(8,128)(2,1)S(1)}, u32[]{:S(2)}, u32[]{:S(2)}) collective-permute-start(bf16[2,128,128]{2,1,0:T(8,128)(2,1)S(1)} %get-tuple-element.24.refs_0_), channel_id=1, source_target_pairs={{8,0},{12,4},{16,8},{20,12},{24,16},{28,20},{0,24},{4,28},{9,1},{1... | collective-permute-start | bytes 196616 | tf_op jit(solution)/shard_map/ppermute | solution.py:23
  6.0 4.6 %collective-permute-start.3 = (bf16[2,128,128]{2,1,0:T(8,128)(2,1)S(1)}, bf16[2,128,128]{2,1,0:T(8,128)(2,1)S(1)}, u32[]{:S(2)}, u32[]{:S(2)}) collective-permute-start(bf16[2,128,128]{2,1,0:T(8,128)(2,1)S(1)} %get-tuple-element.24.refs_0_), channel_id=1, source_target_pairs={{24,0},{28,4},{0,8},{4,12},{8,16},{12,20},{16,24},{20,28},{25,1},{... | collective-permute-start | bytes 196616 | tf_op jit(solution)/shard_map/ppermute | solution.py:23
  7.6 4.7 %collective-permute-start.1 = (bf16[8,32,128]{2,1,0:T(8,128)(2,1)S(1)}, bf16[8,32,128]{2,1,0:T(8,128)(2,1)S(1)}, u32[]{:S(2)}, u32[]{:S(2)}) collective-permute-start(bf16[8,32,128]{2,1,0:T(8,128)(2,1)S(1)} %get-tuple-element.26), channel_id=1, source_target_pairs={{3,0},{0,1},{1,2},{2,3},{7,4},{4,5},{5,6},{6,7},{11,8},{8,9},{9,10... | collective-permute-start | bytes 196616 | tf_op jit(solution)/shard_map/ppermute | solution.py:23
  9.2 5.2 %collective-permute-start.2 = (bf16[8,32,128]{2,1,0:T(8,128)(2,1)S(1)}, bf16[8,32,128]{2,1,0:T(8,128)(2,1)S(1)}, u32[]{:S(2)}, u32[]{:S(2)}) collective-permute-start(bf16[8,32,128]{2,1,0:T(8,128)(2,1)S(1)} %get-tuple-element.27), channel_id=1, source_target_pairs={{1,0},{2,1},{3,2},{0,3},{5,4},{6,5},{7,6},{4,7},{9,8},{10,9},{11,1... | collective-permute-start | bytes 196616 | tf_op jit(solution)/shard_map/ppermute | solution.py:23
  14.4 14.4 %collective-permute-start.8 = (bf16[20,32,128]{2,1,0:T(8,128)(2,1)S(1)}, bf16[20,32,128]{2,1,0:T(8,128)(2,1)S(1)}, u32[]{:S(2)}, u32[]{:S(2)}) collective-permute-start(bf16[20,32,128]{2,1,0:T(8,128)(2,1)S(1)} %get-tuple-element.38), channel_id=1, source_target_pairs={{2,0},{3,1},{0,2},{1,3},{6,4},{7,5},{4,6},{5,7},{10,8},{11,9},{8,1... | collective-permute-start | bytes 491528 | tf_op jit(solution)/shard_map/ppermute | solution.py:23
  16.6 10.0 %collective-permute-start.6 = (bf16[12,32,128]{2,1,0:T(8,128)(2,1)S(1)}, bf16[12,32,128]{2,1,0:T(8,128)(2,1)S(1)}, u32[]{:S(2)}, u32[]{:S(2)}) collective-permute-start(bf16[12,32,128]{2,1,0:T(8,128)(2,1)S(1)} %get-tuple-element.36), channel_id=1, source_target_pairs={{3,0},{0,1},{1,2},{2,3},{7,4},{4,5},{5,6},{6,7},{11,8},{8,9},{9,10... | collective-permute-start | bytes 294920 | tf_op jit(solution)/shard_map/ppermute | solution.py:23
  17.1 11.7 %collective-permute-start.7 = (bf16[12,32,128]{2,1,0:T(8,128)(2,1)S(1)}, bf16[12,32,128]{2,1,0:T(8,128)(2,1)S(1)}, u32[]{:S(2)}, u32[]{:S(2)}) collective-permute-start(bf16[12,32,128]{2,1,0:T(8,128)(2,1)S(1)} %get-tuple-element.37), channel_id=1, source_target_pairs={{1,0},{2,1},{3,2},{0,3},{5,4},{6,5},{7,6},{4,7},{9,8},{10,9},{11,1... | collective-permute-start | bytes 294920 | tf_op jit(solution)/shard_map/ppermute | solution.py:23

commit v3 on v2

--- a/solution.py
+++ b/solution.py
@@ -270,8 +270,10 @@
     near_early = [from_behind(piece, "grp", d) for piece, d in zip(near_early, early)]
     layout = [(0, False)] + [(d, False) for d in early] + [(d, True) for d in late]
     far = galerkin_call(True, layout, share, todo, blocks, flipped, [behind, ahead, across], near_late)
-    if GATE:
-        near_early, far = lax.optimization_barrier((near_early, far))
+    if near_early:
+        *far, last = far
+        near_early, last = lax.optimization_barrier((near_early, last))
+        far = [*far, last]
     far_own, far_early, both = far[0], far[1 : 1 + len(early)], far[1 + len(early) :]
     order = [d for d in ORDER[parts]] if split else []
     moved = {d: from_behind(piece, "grp", d) for d, piece in sorted(
@@ -285,9 +287,8 @@
     )
 
 
-GATE = True
-EARLY = {1: [], 2: [1], 3: [1], 4: [1, 3]}
-LATE = {1: [], 2: [], 3: [2], 4: [2]}
+EARLY = {1: [], 2: [1], 3: [1], 4: [2, 1, 3]}
+LATE = {1: [], 2: [], 3: [2], 4: []}
 ORDER = {1: [], 2: [1], 3: [1, 2], 4: [2, 1, 3]}
 
 

time: 29.9 us -> 27.9 us (0.933)
  the two profiles are of different devices: /device:TPU:10 before, /device:TPU:0 now
where the time goes in v3:
time: 27.9 us; the launch traced here: 27.7 us
  starting transfers between devices  17.1 us (61%)
  Pallas kernels  6.16 us (22%)
  waiting for transfers between devices  3.69 us (13%)
  between operations  0.77 us (3%)
    ppermute x8, starting transfers between devices, from_behind(): lax.ppermute(block, axis, [((i - distance) % size, i) for i in range(size)])  13 us
    ppermute x8, waiting for transfers between devices, from_behind(): lax.ppermute(block, axis, [((i - distance) % size, i) for i in range(size)])  3.68 us
    ppermute x1, starting transfers between devices, from_across(): lax.ppermute(block, 'blk', [((i + (1 if i % 2 else -1)) % size, i) for i...  3.56 us
    pallas_call x2, Pallas kernels, galerkin_call(): pl.pallas_call(functools.partial(galerkin_kernel, far, layout, parts, nnz...  2.71 us
    pallas_call x1, Pallas kernels, prolong_call(): pl.pallas_call(prolong_kernel, out_shape=(jax.ShapeDtypeStruct(tentative....  2.12 us
    pallas_call x1, Pallas kernels, finish_call(): pl.pallas_call(functools.partial(finish_kernel, at_odd, len(near), len(fa...  1.33 us
  transfers between devices with their start and end apart: 10, of which 3 were waited for; matrix products, arithmetic and copies ran while one was open for 0% of the time, Pallas kernels for 10%

profile of v3, /device:TPU:0, one launch (start us, length us, event | category | flops | bytes accessed | tf_op | source)
XLA Modules:
  0.0 27.7 jit_solution(9131837904231796574)
XLA Ops:
  0.0 0.0 copy-start
  0.7 2.1 %prolong.1 = (bf16[2,128,128]{2,1,0:T(8,128)(2,1)S(1)}, bf16[2,128,128]{2,1,0:T(8,128)(2,1)S(1)}, s32[32]{0:T(128)S(1)}) custom-call(s32[1]{0:T(128)S(6)} %copy.7.counts, s32[2,12]{1,0:T(2,128)} %neighbours.1, s32[1,2,8]{2,1,0:T(2,128)} %bitcast.4, bf16[2,12,128,128]{3,2,1,0:T(8,128)(2,1)} %blocks.1, bf16[2,128,128]{2,1,0:T(8,128)(2,1)} %tentative.1, ...), custom_call_target="tpu_custom_call" | custom-call | flops 100000000 | bytes 1000000 | tf_op jit(solution)/shard_map/prolong/pallas_call | solution.py:118
  2.9 0.5 %collective-permute-start = (bf16[2,128,128]{2,1,0:T(8,128)(2,1)S(1)}, bf16[2,128,128]{2,1,0:T(8,128)(2,1)S(1)}, u32[]{:S(2)}, u32[]{:S(2)}) collective-permute-start(bf16[2,128,128]{2,1,0:T(8,128)(2,1)S(1)} %get-tuple-element.22.refs_0_), channel_id=1, source_target_pairs={{4,0},{0,4},{12,8},{8,12},{20,16},{16,20},{28,24},{24,28},{5,1},{1... | collective-permute-start | bytes 196616 | tf_op jit(solution)/shard_map/ppermute | solution.py:28
  3.4 3.6 %collective-permute-start.6 = (bf16[2,128,128]{2,1,0:T(8,128)(2,1)S(1)}, bf16[2,128,128]{2,1,0:T(8,128)(2,1)S(1)}, u32[]{:S(2)}, u32[]{:S(2)}) collective-permute-start(bf16[2,128,128]{2,1,0:T(8,128)(2,1)S(1)} %get-tuple-element.22.refs_0_), channel_id=1, source_target_pairs={{28,0},{8,4},{4,8},{16,12},{12,16},{24,20},{20,24},{0,28},{29,1},{... | collective-permute-start | bytes 196616 | tf_op jit(solution)/shard_map/ppermute | solution.py:33
  6.9 0.5 %collective-permute-start.5 = (bf16[2,128,128]{2,1,0:T(8,128)(2,1)S(1)}, bf16[2,128,128]{2,1,0:T(8,128)(2,1)S(1)}, u32[]{:S(2)}, u32[]{:S(2)}) collective-permute-start(bf16[2,128,128]{2,1,0:T(8,128)(2,1)S(1)} %get-tuple-element.22.refs_0_), channel_id=1, source_target_pairs={{8,0},{12,4},{16,8},{20,12},{24,16},{28,20},{0,24},{4,28},{9,1},{1... | collective-permute-start | bytes 196616 | tf_op jit(solution)/shard_map/ppermute | solution.py:23
  7.5 1.5 %collective-permute-start.4 = (bf16[2,128,128]{2,1,0:T(8,128)(2,1)S(1)}, bf16[2,128,128]{2,1,0:T(8,128)(2,1)S(1)}, u32[]{:S(2)}, u32[]{:S(2)}) collective-permute-start(bf16[2,128,128]{2,1,0:T(8,128)(2,1)S(1)} %get-tuple-element.22.refs_0_), channel_id=1, source_target_pairs={{24,0},{28,4},{0,8},{4,12},{8,16},{12,20},{16,24},{20,28},{25,1},{... | collective-permute-start | bytes 196616 | tf_op jit(solution)/shard_map/ppermute | solution.py:23
  9.0 0.0 collective-permute-done.refs_1_
  9.0 0.0 copy-done
  9.0 1.1 %near.1 = (f32[8,32,128]{2,1,0:T(8,128)S(1)}, bf16[8,32,128]{2,1,0:T(8,128)(2,1)S(1)}, bf16[8,32,128]{2,1,0:T(8,128)(2,1)S(1)}, bf16[8,32,128]{2,1,0:T(8,128)(2,1)S(1)}) custom-call(s32[32]{0:T(128)S(1)} %get-tuple-element.20.todo, bf16[24,128,128]{2,1,0:T(8,128)(2,1)S(1)} %bitcast.2, bf16[2,128,128]{2,1,0:T(8,128)(2,1)S(1)} %get-tuple-element.21.flipped, ...), custom_call_target="tpu_custom_call" | custom-call | flops 200000000 | bytes 2000000 | tf_op jit(solution)/shard_map/near/pallas_call | solution.py:198
  10.1 2.7 %collective-permute-start.1 = (bf16[8,32,128]{2,1,0:T(8,128)(2,1)S(1)}, bf16[8,32,128]{2,1,0:T(8,128)(2,1)S(1)}, u32[]{:S(2)}, u32[]{:S(2)}) collective-permute-start(bf16[8,32,128]{2,1,0:T(8,128)(2,1)S(1)} %get-tuple-element.24), channel_id=1, source_target_pairs={{2,0},{3,1},{0,2},{1,3},{6,4},{7,5},{4,6},{5,7},{10,8},{11,9},{8,1... | collective-permute-start | bytes 196616 | tf_op jit(solution)/shard_map/ppermute | solution.py:23
  12.7 1.6 %collective-permute-start.2 = (bf16[8,32,128]{2,1,0:T(8,128)(2,1)S(1)}, bf16[8,32,128]{2,1,0:T(8,128)(2,1)S(1)}, u32[]{:S(2)}, u32[]{:S(2)}) collective-permute-start(bf16[8,32,128]{2,1,0:T(8,128)(2,1)S(1)} %get-tuple-element.25), channel_id=1, source_target_pairs={{3,0},{0,1},{1,2},{2,3},{7,4},{4,5},{5,6},{6,7},{11,8},{8,9},{9,10... | collective-permute-start | bytes 196616 | tf_op jit(solution)/shard_map/ppermute | solution.py:23
  14.3 0.0 collective-permute-done.6.refs_2_
  14.3 2.2 %collective-permute-start.3 = (bf16[8,32,128]{2,1,0:T(8,128)(2,1)S(1)}, bf16[8,32,128]{2,1,0:T(8,128)(2,1)S(1)}, u32[]{:S(2)}, u32[]{:S(2)}) collective-permute-start(bf16[8,32,128]{2,1,0:T(8,128)(2,1)S(1)} %get-tuple-element.26), channel_id=1, source_target_pairs={{1,0},{2,1},{3,2},{0,3},{5,4},{6,5},{7,6},{4,7},{9,8},{10,9},{11,1... | collective-permute-start | bytes 196616 | tf_op jit(solution)/shard_map/ppermute | solution.py:23
  16.6 0.0 collective-permute-done.5.refs_1_
  16.6 0.0 collective-permute-done.4.refs_0_
  16.6 1.6 %far.1 = (f32[12,32,128]{2,1,0:T(8,128)S(1)}, bf16[12,32,128]{2,1,0:T(8,128)(2,1)S(1)}, bf16[12,32,128]{2,1,0:T(8,128)(2,1)S(1)}, bf16[12,32,128]{2,1,0:T(8,128)(2,1)S(1)}) custom-call(s32[32]{0:T(128)S(1)} %get-tuple-element.20.todo, bf16[24,128,128]{2,1,0:T(8,128)(2,1)S(1)} %bitcast.3, bf16[2,128,128]{2,1,0:T(8,128)(2,1)S(1)} %get-tuple-element.21.flipped, ...), custom_call_target="tpu_custom_call" | custom-call | flops 200000000 | bytes 2000000 | tf_op jit(solution)/shard_map/far/pallas_call | solution.py:198
  18.2 0.1 collective-permute-start.7
  18.3 0.6 %collective-permute-start.8 = (bf16[12,32,128]{2,1,0:T(8,128)(2,1)S(1)}, bf16[12,32,128]{2,1,0:T(8,128)(2,1)S(1)}, u32[]{:S(2)}, u32[]{:S(2)}) collective-permute-start(bf16[12,32,128]{2,1,0:T(8,128)(2,1)S(1)} %get-tuple-element.33), channel_id=1, source_target_pairs={{3,0},{0,1},{1,2},{2,3},{7,4},{4,5},{5,6},{6,7},{11,8},{8,9},{9,10... | collective-permute-start | bytes 294920 | tf_op jit(solution)/shard_map/ppermute | solution.py:23
  18.8 0.0 collective-permute-done.1.refs_1_
  18.8 0.6 %collective-permute-done.2.refs_2_ = bf16[8,32,128]{2,1,0:T(8,128)(2,1)S(1)} collective-permute-done((bf16[8,32,128]{2,1,0:T(8,128)(2,1)S(1)}, bf16[8,32,128]{2,1,0:T(8,128)(2,1)S(1)}, u32[]{:S(2)}, u32[]{:S(2)}) %collective-permute-start.2) | collective-permute-done | bytes 65568 | tf_op jit(solution)/shard_map/ppermute | solution.py:23
  19.4 0.0 collective-permute-done.3.refs_3_
  19.4 3.9 %collective-permute-start.9 = (bf16[12,32,128]{2,1,0:T(8,128)(2,1)S(1)}, bf16[12,32,128]{2,1,0:T(8,128)(2,1)S(1)}, u32[]{:S(2)}, u32[]{:S(2)}) collective-permute-start(bf16[12,32,128]{2,1,0:T(8,128)(2,1)S(1)} %get-tuple-element.34), channel_id=1, source_target_pairs={{1,0},{2,1},{3,2},{0,3},{5,4},{6,5},{7,6},{4,7},{9,8},{10,9},{11,1... | collective-permute-start | bytes 294920 | tf_op jit(solution)/shard_map/ppermute | solution.py:23
  23.3 3.0 %collective-permute-done.7.refs_5_ = bf16[12,32,128]{2,1,0:T(8,128)(2,1)S(1)} collective-permute-done((bf16[12,32,128]{2,1,0:T(8,128)(2,1)S(1)}, bf16[12,32,128]{2,1,0:T(8,128)(2,1)S(1)}, u32[]{:S(2)}, u32[]{:S(2)}) %collective-permute-start.7) | collective-permute-done | bytes 98336 | tf_op jit(solution)/shard_map/ppermute | solution.py:23
  26.3 0.0 collective-permute-done.8.refs_6_
  26.3 0.1 collective-permute-done.9.refs_7_
  26.4 1.3 %finish.1 = f32[2,5,2,32,128]{4,3,2,1,0:T(8,128)} custom-call(s32[32]{0:T(128)S(1)} %get-tuple-element.20.todo, f32[8,32,128]{2,1,0:T(8,128)S(1)} %get-tuple-element.23.refs_0_, bf16[8,32,128]{2,1,0:T(8,128)(2,1)S(1)} %collective-permute-done.1.refs_1_, bf16[8,32,128]{2,1,0:T(8,128)(2,1)S(1)} %collective-permute-done.2.refs_2_, ...), custom_call_target="tpu_custom_call" | custom-call | flops 1000000 | bytes 1500000 | tf_op jit(solution)/shard_map/finish/pallas_call | solution.py:240
Async XLA Ops:
  0.0 9.0 %copy-start = (bf16[2,12,128,128]{3,2,1,0:T(8,128)(2,1)S(1)}, bf16[2,12,128,128]{3,2,1,0:T(8,128)(2,1)}, u32[]{:S(2)}) copy-start(bf16[2,12,128,128]{3,2,1,0:T(8,128)(2,1)} %blocks.1) | copy-start | bytes 2359300
  2.9 6.1 %collective-permute-start = (bf16[2,128,128]{2,1,0:T(8,128)(2,1)S(1)}, bf16[2,128,128]{2,1,0:T(8,128)(2,1)S(1)}, u32[]{:S(2)}, u32[]{:S(2)}) collective-permute-start(bf16[2,128,128]{2,1,0:T(8,128)(2,1)S(1)} %get-tuple-element.22.refs_0_), channel_id=1, source_target_pairs={{4,0},{0,4},{12,8},{8,12},{20,16},{16,20},{28,24},{24,28},{5,1},{1... | collective-permute-start | bytes 196616 | tf_op jit(solution)/shard_map/ppermute | solution.py:28
  3.4 10.9 %collective-permute-start.6 = (bf16[2,128,128]{2,1,0:T(8,128)(2,1)S(1)}, bf16[2,128,128]{2,1,0:T(8,128)(2,1)S(1)}, u32[]{:S(2)}, u32[]{:S(2)}) collective-permute-start(bf16[2,128,128]{2,1,0:T(8,128)(2,1)S(1)} %get-tuple-element.22.refs_0_), channel_id=1, source_target_pairs={{28,0},{8,4},{4,8},{16,12},{12,16},{24,20},{20,24},{0,28},{29,1},{... | collective-permute-start | bytes 196616 | tf_op jit(solution)/shard_map/ppermute | solution.py:33
  6.9 9.6 %collective-permute-start.5 = (bf16[2,128,128]{2,1,0:T(8,128)(2,1)S(1)}, bf16[2,128,128]{2,1,0:T(8,128)(2,1)S(1)}, u32[]{:S(2)}, u32[]{:S(2)}) collective-permute-start(bf16[2,128,128]{2,1,0:T(8,128)(2,1)S(1)} %get-tuple-element.22.refs_0_), channel_id=1, source_target_pairs={{8,0},{12,4},{16,8},{20,12},{24,16},{28,20},{0,24},{4,28},{9,1},{1... | collective-permute-start | bytes 196616 | tf_op jit(solution)/shard_map/ppermute | solution.py:23
  7.5 9.1 %collective-permute-start.4 = (bf16[2,128,128]{2,1,0:T(8,128)(2,1)S(1)}, bf16[2,128,128]{2,1,0:T(8,128)(2,1)S(1)}, u32[]{:S(2)}, u32[]{:S(2)}) collective-permute-start(bf16[2,128,128]{2,1,0:T(8,128)(2,1)S(1)} %get-tuple-element.22.refs_0_), channel_id=1, source_target_pairs={{24,0},{28,4},{0,8},{4,12},{8,16},{12,20},{16,24},{20,28},{25,1},{... | collective-permute-start | bytes 196616 | tf_op jit(solution)/shard_map/ppermute | solution.py:23
  10.1 8.8 %collective-permute-start.1 = (bf16[8,32,128]{2,1,0:T(8,128)(2,1)S(1)}, bf16[8,32,128]{2,1,0:T(8,128)(2,1)S(1)}, u32[]{:S(2)}, u32[]{:S(2)}) collective-permute-start(bf16[8,32,128]{2,1,0:T(8,128)(2,1)S(1)} %get-tuple-element.24), channel_id=1, source_target_pairs={{2,0},{3,1},{0,2},{1,3},{6,4},{7,5},{4,6},{5,7},{10,8},{11,9},{8,1... | collective-permute-start | bytes 196616 | tf_op jit(solution)/shard_map/ppermute | solution.py:23
  12.7 6.7 %collective-permute-start.2 = (bf16[8,32,128]{2,1,0:T(8,128)(2,1)S(1)}, bf16[8,32,128]{2,1,0:T(8,128)(2,1)S(1)}, u32[]{:S(2)}, u32[]{:S(2)}) collective-permute-start(bf16[8,32,128]{2,1,0:T(8,128)(2,1)S(1)} %get-tuple-element.25), channel_id=1, source_target_pairs={{3,0},{0,1},{1,2},{2,3},{7,4},{4,5},{5,6},{6,7},{11,8},{8,9},{9,10... | collective-permute-start | bytes 196616 | tf_op jit(solution)/shard_map/ppermute | solution.py:23
  14.3 5.1 %collective-permute-start.3 = (bf16[8,32,128]{2,1,0:T(8,128)(2,1)S(1)}, bf16[8,32,128]{2,1,0:T(8,128)(2,1)S(1)}, u32[]{:S(2)}, u32[]{:S(2)}) collective-permute-start(bf16[8,32,128]{2,1,0:T(8,128)(2,1)S(1)} %get-tuple-element.26), channel_id=1, source_target_pairs={{1,0},{2,1},{3,2},{0,3},{5,4},{6,5},{7,6},{4,7},{9,8},{10,9},{11,1... | collective-permute-start | bytes 196616 | tf_op jit(solution)/shard_map/ppermute | solution.py:23
  18.2 8.1 %collective-permute-start.7 = (bf16[12,32,128]{2,1,0:T(8,128)(2,1)S(1)}, bf16[12,32,128]{2,1,0:T(8,128)(2,1)S(1)}, u32[]{:S(2)}, u32[]{:S(2)}) collective-permute-start(bf16[12,32,128]{2,1,0:T(8,128)(2,1)S(1)} %get-tuple-element.32), channel_id=1, source_target_pairs={{2,0},{3,1},{0,2},{1,3},{6,4},{7,5},{4,6},{5,7},{10,8},{11,9},{8,1... | collective-permute-start | bytes 294920 | tf_op jit(solution)/shard_map/ppermute | solution.py:23
  18.3 8.0 %collective-permute-start.8 = (bf16[12,32,128]{2,1,0:T(8,128)(2,1)S(1)}, bf16[12,32,128]{2,1,0:T(8,128)(2,1)S(1)}, u32[]{:S(2)}, u32[]{:S(2)}) collective-permute-start(bf16[12,32,128]{2,1,0:T(8,128)(2,1)S(1)} %get-tuple-element.33), channel_id=1, source_target_pairs={{3,0},{0,1},{1,2},{2,3},{7,4},{4,5},{5,6},{6,7},{11,8},{8,9},{9,10... | collective-permute-start | bytes 294920 | tf_op jit(solution)/shard_map/ppermute | solution.py:23
  19.4 6.9 %collective-permute-start.9 = (bf16[12,32,128]{2,1,0:T(8,128)(2,1)S(1)}, bf16[12,32,128]{2,1,0:T(8,128)(2,1)S(1)}, u32[]{:S(2)}, u32[]{:S(2)}) collective-permute-start(bf16[12,32,128]{2,1,0:T(8,128)(2,1)S(1)} %get-tuple-element.34), channel_id=1, source_target_pairs={{1,0},{2,1},{3,2},{0,3},{5,4},{6,5},{7,6},{4,7},{9,8},{10,9},{11,1... | collective-permute-start | bytes 294920 | tf_op jit(solution)/shard_map/ppermute | solution.py:23

commit v4 on v3

--- a/solution.py
+++ b/solution.py
@@ -91,8 +91,6 @@
             todo[at] = (word & ((1 << 30) - 1)) + entry
             near = near + first
     todo[slots * nnz] = near
-    todo[slots * nnz + 1] = odd
-    todo[slots * nnz + 2] = lax.axis_index("grp")
 
     for copy in large[:2]:
         copy.wait()
@@ -178,7 +176,7 @@
         rows = out.shape[1]
         start = 0
         if parts > 1:
-            target = lax.rem(todo[entries + 2] + distance, parts)
+            target = lax.rem(lax.axis_index("grp") + distance, parts)
             start = pl.multiple_of(target * rows, rows)
         skip = out.shape[0] - dests
         if carry:
@@ -213,11 +211,11 @@
     )(todo, blocks.reshape(slots * nnz, pores, pores), flipped, *halo, *carried)
 
 
-def finish_kernel(at_odd, nears, fars, boths, todo, *refs):
+def finish_kernel(nears, fars, boths, *refs):
     near, refs = refs[:nears], refs[nears:]
     far, refs = refs[:fars], refs[fars:]
-    both, out = refs[:boths], refs[boths]
-    odd = todo[at_odd] == 1
+    both, (out, held, sem) = refs[:boths], refs[boths:]
+    odd = lax.rem(lax.axis_index("blk"), 2) == 1
     skip = NCG * NEAR * NCG
     for pieces, panels, first in ((near, NEAR, 0), (far, FAR, skip)):
         for c in range(NCG):
@@ -226,26 +224,33 @@
                     offset = jnp.where(odd, 1, 3) if panel else 2
                 else:
                     offset = (0, 4, jnp.where(odd, 3, 1))[panel]
+                base = (c * panels + panel) * NCG
                 for c2 in range(NCG):
-                    dest = (c * panels + panel) * NCG + c2
+                    dest = base + c2
                     total = pieces[0][dest].astype(jnp.float32)
                     for piece in pieces[1:]:
                         total = total + piece[dest].astype(jnp.float32)
                     for piece in both:
                         total = total + piece[first + dest].astype(jnp.float32)
-                    out[c, offset, c2] = total
-
-
-def finish_call(at_odd, todo, near, far, both, rows, width):
+                    held[first + dest] = total
+                pltpu.make_async_copy(held.at[pl.ds(first + base, NCG)], out.at[c, offset], sem).start()
+    pltpu.make_async_copy(held, held, sem).wait()
+
+
+def finish_call(near, far, both, rows, width):
     return pl.pallas_call(
-        functools.partial(finish_kernel, at_odd, len(near), len(far), len(both)),
+        functools.partial(finish_kernel, len(near), len(far), len(both)),
         out_shape=jax.ShapeDtypeStruct((NCG, OFFSETS, NCG, rows, width), jnp.float32),
-        in_specs=[SMEM] + [VMEM] * (len(near) + len(far) + len(both)),
-        out_specs=VMEM,
+        in_specs=[VMEM] * (len(near) + len(far) + len(both)),
+        out_specs=ANY,
+        scratch_shapes=[
+            pltpu.VMEM((NCG * OFFSETS * NCG, rows, width), jnp.float32),
+            pltpu.SemaphoreType.DMA,
+        ],
         compiler_params=pltpu.CompilerParams(vmem_limit_bytes=16 << 20),
         cost_estimate=pl.CostEstimate(flops=1_000_000, bytes_accessed=1_500_000, transcendentals=0),
         name="finish",
-    )(todo, *near, *far, *both)
+    )(*near, *far, *both)
 
 
 def local(blocks, neighbours, tentative, inv_diag, coarse_map, counts):
@@ -283,7 +288,7 @@
     if not split:
         near_own, far_own = gathered(near_own, parts), gathered(far_own, parts)
     return finish_call(
-        slots * nnz + 1, todo, [near_own] + near_early, [far_own] + far_early, both, width // parts, width
+        [near_own] + near_early, [far_own] + far_early, both, width // parts, width
     )
 
 

time: 27.9 us -> 27.5 us (0.986)
  Pallas kernels: 6.16 us -> 5.57 us
    pallas_call x1, Pallas kernels: 1.33 us -> 0.73 us  [finish_call(): pl.pallas_call(functools.partial(finish_kernel, len(near), len(far), len(...]
where the time goes in v4:
time: 27.5 us; the launch traced here: 27.2 us
  starting transfers between devices  17.3 us (63%)
  Pallas kernels  5.57 us (20%)
  waiting for transfers between devices  3.58 us (13%)
  between operations  0.77 us (3%)
    ppermute x8, starting transfers between devices, from_behind(): lax.ppermute(block, axis, [((i - distance) % size, i) for i in range(size)])  13.2 us
    ppermute x8, waiting for transfers between devices, from_behind(): lax.ppermute(block, axis, [((i - distance) % size, i) for i in range(size)])  3.57 us
    ppermute x1, starting transfers between devices, from_across(): lax.ppermute(block, 'blk', [((i + (1 if i % 2 else -1)) % size, i) for i...  3.56 us
    pallas_call x2, Pallas kernels, galerkin_call(): pl.pallas_call(functools.partial(galerkin_kernel, far, layout, parts, nnz...  2.72 us
    pallas_call x1, Pallas kernels, prolong_call(): pl.pallas_call(prolong_kernel, out_shape=(jax.ShapeDtypeStruct(tentative....  2.12 us
    pallas_call x1, Pallas kernels, finish_call(): pl.pallas_call(functools.partial(finish_kernel, len(near), len(far), len(...  0.73 us
  transfers between devices with their start and end apart: 10, of which 3 were waited for; matrix products, arithmetic and copies ran while one was open for 0% of the time, Pallas kernels for 10%

profile of v4, /device:TPU:0, one launch (start us, length us, event | category | flops | bytes accessed | tf_op | source)
XLA Modules:
  0.0 27.2 jit_solution(9264867735850993388)
XLA Ops:
  0.0 0.0 copy-start
  0.7 2.1 %prolong.1 = (bf16[2,128,128]{2,1,0:T(8,128)(2,1)S(1)}, bf16[2,128,128]{2,1,0:T(8,128)(2,1)S(1)}, s32[32]{0:T(128)S(1)}) custom-call(s32[1]{0:T(128)S(6)} %copy.7.counts, s32[2,12]{1,0:T(2,128)} %neighbours.1, s32[1,2,8]{2,1,0:T(2,128)} %bitcast.4, bf16[2,12,128,128]{3,2,1,0:T(8,128)(2,1)} %blocks.1, bf16[2,128,128]{2,1,0:T(8,128)(2,1)} %tentative.1, ...), custom_call_target="tpu_custom_call" | custom-call | flops 100000000 | bytes 1000000 | tf_op jit(solution)/shard_map/prolong/pallas_call | solution.py:116
  2.9 0.5 %collective-permute-start = (bf16[2,128,128]{2,1,0:T(8,128)(2,1)S(1)}, bf16[2,128,128]{2,1,0:T(8,128)(2,1)S(1)}, u32[]{:S(2)}, u32[]{:S(2)}) collective-permute-start(bf16[2,128,128]{2,1,0:T(8,128)(2,1)S(1)} %get-tuple-element.22.refs_0_), channel_id=1, source_target_pairs={{4,0},{0,4},{12,8},{8,12},{20,16},{16,20},{28,24},{24,28},{5,1},{1... | collective-permute-start | bytes 196616 | tf_op jit(solution)/shard_map/ppermute | solution.py:28
  3.4 3.6 %collective-permute-start.6 = (bf16[2,128,128]{2,1,0:T(8,128)(2,1)S(1)}, bf16[2,128,128]{2,1,0:T(8,128)(2,1)S(1)}, u32[]{:S(2)}, u32[]{:S(2)}) collective-permute-start(bf16[2,128,128]{2,1,0:T(8,128)(2,1)S(1)} %get-tuple-element.22.refs_0_), channel_id=1, source_target_pairs={{28,0},{8,4},{4,8},{16,12},{12,16},{24,20},{20,24},{0,28},{29,1},{... | collective-permute-start | bytes 196616 | tf_op jit(solution)/shard_map/ppermute | solution.py:33
  6.9 0.5 %collective-permute-start.5 = (bf16[2,128,128]{2,1,0:T(8,128)(2,1)S(1)}, bf16[2,128,128]{2,1,0:T(8,128)(2,1)S(1)}, u32[]{:S(2)}, u32[]{:S(2)}) collective-permute-start(bf16[2,128,128]{2,1,0:T(8,128)(2,1)S(1)} %get-tuple-element.22.refs_0_), channel_id=1, source_target_pairs={{8,0},{12,4},{16,8},{20,12},{24,16},{28,20},{0,24},{4,28},{9,1},{1... | collective-permute-start | bytes 196616 | tf_op jit(solution)/shard_map/ppermute | solution.py:23
  7.5 1.5 %collective-permute-start.4 = (bf16[2,128,128]{2,1,0:T(8,128)(2,1)S(1)}, bf16[2,128,128]{2,1,0:T(8,128)(2,1)S(1)}, u32[]{:S(2)}, u32[]{:S(2)}) collective-permute-start(bf16[2,128,128]{2,1,0:T(8,128)(2,1)S(1)} %get-tuple-element.22.refs_0_), channel_id=1, source_target_pairs={{24,0},{28,4},{0,8},{4,12},{8,16},{12,20},{16,24},{20,28},{25,1},{... | collective-permute-start | bytes 196616 | tf_op jit(solution)/shard_map/ppermute | solution.py:23
  9.0 0.0 collective-permute-done.refs_1_
  9.0 0.0 copy-done
  9.0 1.1 %near.1 = (f32[8,32,128]{2,1,0:T(8,128)S(1)}, bf16[8,32,128]{2,1,0:T(8,128)(2,1)S(1)}, bf16[8,32,128]{2,1,0:T(8,128)(2,1)S(1)}, bf16[8,32,128]{2,1,0:T(8,128)(2,1)S(1)}) custom-call(s32[32]{0:T(128)S(1)} %get-tuple-element.20.todo, bf16[24,128,128]{2,1,0:T(8,128)(2,1)S(1)} %bitcast.2, bf16[2,128,128]{2,1,0:T(8,128)(2,1)S(1)} %get-tuple-element.21.flipped, ...), custom_call_target="tpu_custom_call" | custom-call | flops 200000000 | bytes 2000000 | tf_op jit(solution)/shard_map/near/pallas_call | solution.py:196
  10.1 2.7 %collective-permute-start.1 = (bf16[8,32,128]{2,1,0:T(8,128)(2,1)S(1)}, bf16[8,32,128]{2,1,0:T(8,128)(2,1)S(1)}, u32[]{:S(2)}, u32[]{:S(2)}) collective-permute-start(bf16[8,32,128]{2,1,0:T(8,128)(2,1)S(1)} %get-tuple-element.24), channel_id=1, source_target_pairs={{2,0},{3,1},{0,2},{1,3},{6,4},{7,5},{4,6},{5,7},{10,8},{11,9},{8,1... | collective-permute-start | bytes 196616 | tf_op jit(solution)/shard_map/ppermute | solution.py:23
  12.7 1.6 %collective-permute-start.2 = (bf16[8,32,128]{2,1,0:T(8,128)(2,1)S(1)}, bf16[8,32,128]{2,1,0:T(8,128)(2,1)S(1)}, u32[]{:S(2)}, u32[]{:S(2)}) collective-permute-start(bf16[8,32,128]{2,1,0:T(8,128)(2,1)S(1)} %get-tuple-element.25), channel_id=1, source_target_pairs={{3,0},{0,1},{1,2},{2,3},{7,4},{4,5},{5,6},{6,7},{11,8},{8,9},{9,10... | collective-permute-start | bytes 196616 | tf_op jit(solution)/shard_map/ppermute | solution.py:23
  14.3 0.0 collective-permute-done.6.refs_2_
  14.3 2.2 %collective-permute-start.3 = (bf16[8,32,128]{2,1,0:T(8,128)(2,1)S(1)}, bf16[8,32,128]{2,1,0:T(8,128)(2,1)S(1)}, u32[]{:S(2)}, u32[]{:S(2)}) collective-permute-start(bf16[8,32,128]{2,1,0:T(8,128)(2,1)S(1)} %get-tuple-element.26), channel_id=1, source_target_pairs={{1,0},{2,1},{3,2},{0,3},{5,4},{6,5},{7,6},{4,7},{9,8},{10,9},{11,1... | collective-permute-start | bytes 196616 | tf_op jit(solution)/shard_map/ppermute | solution.py:23
  16.6 0.0 collective-permute-done.5.refs_1_
  16.6 0.0 collective-permute-done.4.refs_0_
  16.6 1.6 %far.1 = (f32[12,32,128]{2,1,0:T(8,128)S(1)}, bf16[12,32,128]{2,1,0:T(8,128)(2,1)S(1)}, bf16[12,32,128]{2,1,0:T(8,128)(2,1)S(1)}, bf16[12,32,128]{2,1,0:T(8,128)(2,1)S(1)}) custom-call(s32[32]{0:T(128)S(1)} %get-tuple-element.20.todo, bf16[24,128,128]{2,1,0:T(8,128)(2,1)S(1)} %bitcast.3, bf16[2,128,128]{2,1,0:T(8,128)(2,1)S(1)} %get-tuple-element.21.flipped, ...), custom_call_target="tpu_custom_call" | custom-call | flops 200000000 | bytes 2000000 | tf_op jit(solution)/shard_map/far/pallas_call | solution.py:196
  18.2 0.1 collective-permute-start.7
  18.3 0.6 %collective-permute-start.8 = (bf16[12,32,128]{2,1,0:T(8,128)(2,1)S(1)}, bf16[12,32,128]{2,1,0:T(8,128)(2,1)S(1)}, u32[]{:S(2)}, u32[]{:S(2)}) collective-permute-start(bf16[12,32,128]{2,1,0:T(8,128)(2,1)S(1)} %get-tuple-element.33), channel_id=1, source_target_pairs={{3,0},{0,1},{1,2},{2,3},{7,4},{4,5},{5,6},{6,7},{11,8},{8,9},{9,10... | collective-permute-start | bytes 294920 | tf_op jit(solution)/shard_map/ppermute | solution.py:23
  18.8 0.0 collective-permute-done.1.refs_1_
  18.8 0.1 collective-permute-done.2.refs_2_
  19.0 0.3 %collective-permute-done.3.refs_3_ = bf16[8,32,128]{2,1,0:T(8,128)(2,1)S(1)} collective-permute-done((bf16[8,32,128]{2,1,0:T(8,128)(2,1)S(1)}, bf16[8,32,128]{2,1,0:T(8,128)(2,1)S(1)}, u32[]{:S(2)}, u32[]{:S(2)}) %collective-permute-start.3) | collective-permute-done | bytes 65568 | tf_op jit(solution)/shard_map/ppermute | solution.py:23
  19.3 4.1 %collective-permute-start.9 = (bf16[12,32,128]{2,1,0:T(8,128)(2,1)S(1)}, bf16[12,32,128]{2,1,0:T(8,128)(2,1)S(1)}, u32[]{:S(2)}, u32[]{:S(2)}) collective-permute-start(bf16[12,32,128]{2,1,0:T(8,128)(2,1)S(1)} %get-tuple-element.34), channel_id=1, source_target_pairs={{1,0},{2,1},{3,2},{0,3},{5,4},{6,5},{7,6},{4,7},{9,8},{10,9},{11,1... | collective-permute-start | bytes 294920 | tf_op jit(solution)/shard_map/ppermute | solution.py:23
  23.3 3.1 %collective-permute-done.7.refs_5_ = bf16[12,32,128]{2,1,0:T(8,128)(2,1)S(1)} collective-permute-done((bf16[12,32,128]{2,1,0:T(8,128)(2,1)S(1)}, bf16[12,32,128]{2,1,0:T(8,128)(2,1)S(1)}, u32[]{:S(2)}, u32[]{:S(2)}) %collective-permute-start.7) | collective-permute-done | bytes 98336 | tf_op jit(solution)/shard_map/ppermute | solution.py:23
  26.5 0.0 collective-permute-done.8.refs_6_
  26.5 0.0 collective-permute-done.9.refs_7_
  26.5 0.7 %finish.1 = f32[2,5,2,32,128]{4,3,2,1,0:T(8,128)} custom-call(f32[8,32,128]{2,1,0:T(8,128)S(1)} %get-tuple-element.23.refs_0_, bf16[8,32,128]{2,1,0:T(8,128)(2,1)S(1)} %collective-permute-done.1.refs_1_, bf16[8,32,128]{2,1,0:T(8,128)(2,1)S(1)} %collective-permute-done.2.refs_2_, bf16[8,32,128]{2,1,0:T(8,128)(2,1)S(1)} %collective-permute-done.3.refs_3_, ...), custom_call_target="tpu_custom_call" | custom-call | flops 1000000 | bytes 1500000 | tf_op jit(solution)/shard_map/finish/pallas_call | solution.py:241
Async XLA Ops:
  0.0 9.0 %copy-start = (bf16[2,12,128,128]{3,2,1,0:T(8,128)(2,1)S(1)}, bf16[2,12,128,128]{3,2,1,0:T(8,128)(2,1)}, u32[]{:S(2)}) copy-start(bf16[2,12,128,128]{3,2,1,0:T(8,128)(2,1)} %blocks.1) | copy-start | bytes 2359300
  2.9 6.1 %collective-permute-start = (bf16[2,128,128]{2,1,0:T(8,128)(2,1)S(1)}, bf16[2,128,128]{2,1,0:T(8,128)(2,1)S(1)}, u32[]{:S(2)}, u32[]{:S(2)}) collective-permute-start(bf16[2,128,128]{2,1,0:T(8,128)(2,1)S(1)} %get-tuple-element.22.refs_0_), channel_id=1, source_target_pairs={{4,0},{0,4},{12,8},{8,12},{20,16},{16,20},{28,24},{24,28},{5,1},{1... | collective-permute-start | bytes 196616 | tf_op jit(solution)/shard_map/ppermute | solution.py:28
  3.4 10.9 %collective-permute-start.6 = (bf16[2,128,128]{2,1,0:T(8,128)(2,1)S(1)}, bf16[2,128,128]{2,1,0:T(8,128)(2,1)S(1)}, u32[]{:S(2)}, u32[]{:S(2)}) collective-permute-start(bf16[2,128,128]{2,1,0:T(8,128)(2,1)S(1)} %get-tuple-element.22.refs_0_), channel_id=1, source_target_pairs={{28,0},{8,4},{4,8},{16,12},{12,16},{24,20},{20,24},{0,28},{29,1},{... | collective-permute-start | bytes 196616 | tf_op jit(solution)/shard_map/ppermute | solution.py:33
  6.9 9.6 %collective-permute-start.5 = (bf16[2,128,128]{2,1,0:T(8,128)(2,1)S(1)}, bf16[2,128,128]{2,1,0:T(8,128)(2,1)S(1)}, u32[]{:S(2)}, u32[]{:S(2)}) collective-permute-start(bf16[2,128,128]{2,1,0:T(8,128)(2,1)S(1)} %get-tuple-element.22.refs_0_), channel_id=1, source_target_pairs={{8,0},{12,4},{16,8},{20,12},{24,16},{28,20},{0,24},{4,28},{9,1},{1... | collective-permute-start | bytes 196616 | tf_op jit(solution)/shard_map/ppermute | solution.py:23
  7.5 9.1 %collective-permute-start.4 = (bf16[2,128,128]{2,1,0:T(8,128)(2,1)S(1)}, bf16[2,128,128]{2,1,0:T(8,128)(2,1)S(1)}, u32[]{:S(2)}, u32[]{:S(2)}) collective-permute-start(bf16[2,128,128]{2,1,0:T(8,128)(2,1)S(1)} %get-tuple-element.22.refs_0_), channel_id=1, source_target_pairs={{24,0},{28,4},{0,8},{4,12},{8,16},{12,20},{16,24},{20,28},{25,1},{... | collective-permute-start | bytes 196616 | tf_op jit(solution)/shard_map/ppermute | solution.py:23
  10.1 8.8 %collective-permute-start.1 = (bf16[8,32,128]{2,1,0:T(8,128)(2,1)S(1)}, bf16[8,32,128]{2,1,0:T(8,128)(2,1)S(1)}, u32[]{:S(2)}, u32[]{:S(2)}) collective-permute-start(bf16[8,32,128]{2,1,0:T(8,128)(2,1)S(1)} %get-tuple-element.24), channel_id=1, source_target_pairs={{2,0},{3,1},{0,2},{1,3},{6,4},{7,5},{4,6},{5,7},{10,8},{11,9},{8,1... | collective-permute-start | bytes 196616 | tf_op jit(solution)/shard_map/ppermute | solution.py:23
  12.7 6.3 %collective-permute-start.2 = (bf16[8,32,128]{2,1,0:T(8,128)(2,1)S(1)}, bf16[8,32,128]{2,1,0:T(8,128)(2,1)S(1)}, u32[]{:S(2)}, u32[]{:S(2)}) collective-permute-start(bf16[8,32,128]{2,1,0:T(8,128)(2,1)S(1)} %get-tuple-element.25), channel_id=1, source_target_pairs={{3,0},{0,1},{1,2},{2,3},{7,4},{4,5},{5,6},{6,7},{11,8},{8,9},{9,10... | collective-permute-start | bytes 196616 | tf_op jit(solution)/shard_map/ppermute | solution.py:23
  14.3 5.0 %collective-permute-start.3 = (bf16[8,32,128]{2,1,0:T(8,128)(2,1)S(1)}, bf16[8,32,128]{2,1,0:T(8,128)(2,1)S(1)}, u32[]{:S(2)}, u32[]{:S(2)}) collective-permute-start(bf16[8,32,128]{2,1,0:T(8,128)(2,1)S(1)} %get-tuple-element.26), channel_id=1, source_target_pairs={{1,0},{2,1},{3,2},{0,3},{5,4},{6,5},{7,6},{4,7},{9,8},{10,9},{11,1... | collective-permute-start | bytes 196616 | tf_op jit(solution)/shard_map/ppermute | solution.py:23
  18.2 8.3 %collective-permute-start.7 = (bf16[12,32,128]{2,1,0:T(8,128)(2,1)S(1)}, bf16[12,32,128]{2,1,0:T(8,128)(2,1)S(1)}, u32[]{:S(2)}, u32[]{:S(2)}) collective-permute-start(bf16[12,32,128]{2,1,0:T(8,128)(2,1)S(1)} %get-tuple-element.32), channel_id=1, source_target_pairs={{2,0},{3,1},{0,2},{1,3},{6,4},{7,5},{4,6},{5,7},{10,8},{11,9},{8,1... | collective-permute-start | bytes 294920 | tf_op jit(solution)/shard_map/ppermute | solution.py:23
  18.3 8.2 %collective-permute-start.8 = (bf16[12,32,128]{2,1,0:T(8,128)(2,1)S(1)}, bf16[12,32,128]{2,1,0:T(8,128)(2,1)S(1)}, u32[]{:S(2)}, u32[]{:S(2)}) collective-permute-start(bf16[12,32,128]{2,1,0:T(8,128)(2,1)S(1)} %get-tuple-element.33), channel_id=1, source_target_pairs={{3,0},{0,1},{1,2},{2,3},{7,4},{4,5},{5,6},{6,7},{11,8},{8,9},{9,10... | collective-permute-start | bytes 294920 | tf_op jit(solution)/shard_map/ppermute | solution.py:23
  19.3 7.2 %collective-permute-start.9 = (bf16[12,32,128]{2,1,0:T(8,128)(2,1)S(1)}, bf16[12,32,128]{2,1,0:T(8,128)(2,1)S(1)}, u32[]{:S(2)}, u32[]{:S(2)}) collective-permute-start(bf16[12,32,128]{2,1,0:T(8,128)(2,1)S(1)} %get-tuple-element.34), channel_id=1, source_target_pairs={{1,0},{2,1},{3,2},{0,3},{5,4},{6,5},{7,6},{4,7},{9,8},{10,9},{11,1... | collective-permute-start | bytes 294920 | tf_op jit(solution)/shard_map/ppermute | solution.py:23

commit v5 on v4

--- a/solution.py
+++ b/solution.py
@@ -44,7 +44,7 @@
     large = [
         pltpu.make_async_copy(tentative, base.at[pl.ds(0, slots)], sems.at[2]),
         pltpu.make_async_copy(inv_diag, scale, sems.at[3]),
-    ] + [pltpu.make_async_copy(blocks.at[row], held.at[row], sems.at[4 + row]) for row in range(slots)]
+    ] + [pltpu.make_async_copy(blocks, held, sems.at[4])]
     for copy in small + large:
         copy.start()
     base[slots] = jnp.zeros_like(base[slots])
@@ -96,7 +96,8 @@
         copy.wait()
     width = out.shape[2]
     for row in range(slots):
-        large[2 + row].wait()
+        if row == 0:
+            large[2].wait()
         total = None
         for n in range(nnz):
             term = jnp.dot(held[row, n], base[kept[row * nnz + n]], preferred_element_type=jnp.float32)
@@ -129,7 +130,7 @@
             pltpu.SMEM(neighbours.shape, jnp.int32),
             pltpu.SMEM(coarse_map.shape, jnp.int32),
             pltpu.SMEM((slots * OFFSETS * slots,), jnp.int32),
-            pltpu.SemaphoreType.DMA((4 + slots,)),
+            pltpu.SemaphoreType.DMA((5,)),
         ],
         compiler_params=pltpu.CompilerParams(vmem_limit_bytes=16 << 20),
         cost_estimate=pl.CostEstimate(flops=100_000_000, bytes_accessed=1_000_000, transcendentals=0),
@@ -137,11 +138,14 @@
     )(counts, *arrays)
 
 
-def galerkin_kernel(far, layout, parts, nnz, todo, blocks, flipped, *refs):
+def galerkin_kernel(far, layout, parts, nnz, words, blocks, flipped, *refs):
     slots = flipped.shape[0]
     panels = FAR if far else NEAR
     dests = NCG * panels * NCG
     halo, refs = refs[:panels], refs[panels:]
+    *refs, todo, sem = refs
+    list_copy = pltpu.make_async_copy(words, todo, sem)
+    list_copy.start()
     carried, refs = refs[: sum(carry for _, carry in layout)], refs[sum(carry for _, carry in layout) :]
     outs, (pool, acc) = refs[: len(layout)], refs[len(layout) :]
     for panel in range(panels):
@@ -149,13 +153,16 @@
             pool[panel * slots + slot] = halo[panel][slot]
     acc[...] = jnp.zeros_like(acc)
     entries = slots * nnz
+    list_copy.wait()
     near = todo[entries]
     count = entries - near if far else near
 
+    batch = nnz
+
     def some(step, carry):
         grams, places = [], []
-        for j in range(nnz):
-            at = step * nnz + j
+        for j in range(batch):
+            at = step * batch + j
             word = todo[entries - 1 - at if far else at]
             dest = lax.shift_right_logical(word, 16)
             panel = lax.shift_right_logical(word, 8) & 255
@@ -170,7 +177,11 @@
             acc[place] = acc[place] + gram
         return carry
 
-    lax.fori_loop(0, lax.div(count + nnz - 1, nnz), some, 0)
+    if far:
+        for step in range(entries // batch):
+            some(step, 0)
+    else:
+        lax.fori_loop(0, lax.div(count + batch - 1, batch), some, 0)
 
     for (distance, carry), out in zip(layout, outs):
         rows = out.shape[1]
@@ -199,11 +210,13 @@
             jax.ShapeDtypeStruct((skip + dests, rows, width), flipped.dtype if distance else jnp.float32)
             for (distance, _), skip in zip(layout, before)
         ],
-        in_specs=[SMEM, VMEM, VMEM] + [VMEM] * (len(halo) + len(carried)),
+        in_specs=[pl.BlockSpec(memory_space=pl.ANY), VMEM, VMEM] + [VMEM] * (len(halo) + len(carried)),
         out_specs=[VMEM] * len(layout),
         scratch_shapes=[
             pltpu.VMEM((panels * slots, pores, width), flipped.dtype),
             pltpu.VMEM((dests + 1, width, width), jnp.float32),
+            pltpu.SMEM(todo.shape, jnp.int32),
+            pltpu.SemaphoreType.DMA,
         ],
         compiler_params=pltpu.CompilerParams(vmem_limit_bytes=24 << 20),
         cost_estimate=pl.CostEstimate(flops=200_000_000, bytes_accessed=2_000_000, transcendentals=0),

time: 27.5 us -> 27.2 us (0.989)
  Pallas kernels: 5.57 us -> 5.1 us
    pallas_call x2, Pallas kernels: 2.72 us -> 2.37 us  [galerkin_call(): pl.pallas_call(functools.partial(galerkin_kernel, far, layout, parts, nnz...]
  transfers between devices with their start and end apart: 10 -> 10, of which waited for: 3 -> 2; matrix products, arithmetic and copies ran while one was open for 0% -> 0% of each run, Pallas kernels for 10% -> 9%
where the time goes in v5:
time: 27.2 us; the launch traced here: 26.8 us
  starting transfers between devices  17.2 us (63%)
  Pallas kernels  5.1 us (19%)
  waiting for transfers between devices  3.7 us (14%)
  between operations  0.77 us (3%)
    ppermute x8, starting transfers between devices, from_behind(): lax.ppermute(block, axis, [((i - distance) % size, i) for i in range(size)])  13.1 us
    ppermute x8, waiting for transfers between devices, from_behind(): lax.ppermute(block, axis, [((i - distance) % size, i) for i in range(size)])  3.7 us
    ppermute x1, starting transfers between devices, from_across(): lax.ppermute(block, 'blk', [((i + (1 if i % 2 else -1)) % size, i) for i...  3.56 us
    pallas_call x2, Pallas kernels, galerkin_call(): pl.pallas_call(functools.partial(galerkin_kernel, far, layout, parts, nnz...  2.37 us
    pallas_call x1, Pallas kernels, prolong_call(): pl.pallas_call(prolong_kernel, out_shape=(jax.ShapeDtypeStruct(tentative....  2 us
    pallas_call x1, Pallas kernels, finish_call(): pl.pallas_call(functools.partial(finish_kernel, len(near), len(far), len(...  0.73 us
  transfers between devices with their start and end apart: 10, of which 2 were waited for; matrix products, arithmetic and copies ran while one was open for 0% of the time, Pallas kernels for 9%

profile of v5, /device:TPU:0, one launch (start us, length us, event | category | flops | bytes accessed | tf_op | source)
XLA Modules:
  0.0 26.8 jit_solution(6360428774115175105)
XLA Ops:
  0.0 0.0 copy-start
  0.7 2.0 %prolong.1 = (bf16[2,128,128]{2,1,0:T(8,128)(2,1)S(1)}, bf16[2,128,128]{2,1,0:T(8,128)(2,1)S(1)}, s32[32]{0:T(128)S(1)}) custom-call(s32[1]{0:T(128)S(6)} %copy.7.counts, s32[2,12]{1,0:T(2,128)} %neighbours.1, s32[1,2,8]{2,1,0:T(2,128)} %bitcast.4, bf16[2,12,128,128]{3,2,1,0:T(8,128)(2,1)} %blocks.1, bf16[2,128,128]{2,1,0:T(8,128)(2,1)} %tentative.1, ...), custom_call_target="tpu_custom_call" | custom-call | flops 100000000 | bytes 1000000 | tf_op jit(solution)/shard_map/prolong/pallas_call | solution.py:117
  2.7 0.5 %collective-permute-start = (bf16[2,128,128]{2,1,0:T(8,128)(2,1)S(1)}, bf16[2,128,128]{2,1,0:T(8,128)(2,1)S(1)}, u32[]{:S(2)}, u32[]{:S(2)}) collective-permute-start(bf16[2,128,128]{2,1,0:T(8,128)(2,1)S(1)} %get-tuple-element.22.refs_0_), channel_id=1, source_target_pairs={{4,0},{0,4},{12,8},{8,12},{20,16},{16,20},{28,24},{24,28},{5,1},{1... | collective-permute-start | bytes 196616 | tf_op jit(solution)/shard_map/ppermute | solution.py:28
  3.3 3.6 %collective-permute-start.6 = (bf16[2,128,128]{2,1,0:T(8,128)(2,1)S(1)}, bf16[2,128,128]{2,1,0:T(8,128)(2,1)S(1)}, u32[]{:S(2)}, u32[]{:S(2)}) collective-permute-start(bf16[2,128,128]{2,1,0:T(8,128)(2,1)S(1)} %get-tuple-element.22.refs_0_), channel_id=1, source_target_pairs={{28,0},{8,4},{4,8},{16,12},{12,16},{24,20},{20,24},{0,28},{29,1},{... | collective-permute-start | bytes 196616 | tf_op jit(solution)/shard_map/ppermute | solution.py:33
  6.8 0.5 %collective-permute-start.5 = (bf16[2,128,128]{2,1,0:T(8,128)(2,1)S(1)}, bf16[2,128,128]{2,1,0:T(8,128)(2,1)S(1)}, u32[]{:S(2)}, u32[]{:S(2)}) collective-permute-start(bf16[2,128,128]{2,1,0:T(8,128)(2,1)S(1)} %get-tuple-element.22.refs_0_), channel_id=1, source_target_pairs={{8,0},{12,4},{16,8},{20,12},{24,16},{28,20},{0,24},{4,28},{9,1},{1... | collective-permute-start | bytes 196616 | tf_op jit(solution)/shard_map/ppermute | solution.py:23
  7.3 1.5 %collective-permute-start.4 = (bf16[2,128,128]{2,1,0:T(8,128)(2,1)S(1)}, bf16[2,128,128]{2,1,0:T(8,128)(2,1)S(1)}, u32[]{:S(2)}, u32[]{:S(2)}) collective-permute-start(bf16[2,128,128]{2,1,0:T(8,128)(2,1)S(1)} %get-tuple-element.22.refs_0_), channel_id=1, source_target_pairs={{24,0},{28,4},{0,8},{4,12},{8,16},{12,20},{16,24},{20,28},{25,1},{... | collective-permute-start | bytes 196616 | tf_op jit(solution)/shard_map/ppermute | solution.py:23
  8.8 0.0 collective-permute-done.refs_1_
  8.8 0.0 copy-done
  8.8 1.1 %near.1 = (f32[8,32,128]{2,1,0:T(8,128)S(1)}, bf16[8,32,128]{2,1,0:T(8,128)(2,1)S(1)}, bf16[8,32,128]{2,1,0:T(8,128)(2,1)S(1)}, bf16[8,32,128]{2,1,0:T(8,128)(2,1)S(1)}) custom-call(s32[32]{0:T(128)S(1)} %get-tuple-element.20.words, bf16[24,128,128]{2,1,0:T(8,128)(2,1)S(1)} %bitcast.2, bf16[2,128,128]{2,1,0:T(8,128)(2,1)S(1)} %get-tuple-element.21.flipped, ...), custom_call_target="tpu_custom_call" | custom-call | flops 200000000 | bytes 2000000 | tf_op jit(solution)/shard_map/near/pallas_call | solution.py:207
  9.9 2.7 %collective-permute-start.1 = (bf16[8,32,128]{2,1,0:T(8,128)(2,1)S(1)}, bf16[8,32,128]{2,1,0:T(8,128)(2,1)S(1)}, u32[]{:S(2)}, u32[]{:S(2)}) collective-permute-start(bf16[8,32,128]{2,1,0:T(8,128)(2,1)S(1)} %get-tuple-element.24), channel_id=1, source_target_pairs={{2,0},{3,1},{0,2},{1,3},{6,4},{7,5},{4,6},{5,7},{10,8},{11,9},{8,1... | collective-permute-start | bytes 196616 | tf_op jit(solution)/shard_map/ppermute | solution.py:23
  12.6 1.6 %collective-permute-start.2 = (bf16[8,32,128]{2,1,0:T(8,128)(2,1)S(1)}, bf16[8,32,128]{2,1,0:T(8,128)(2,1)S(1)}, u32[]{:S(2)}, u32[]{:S(2)}) collective-permute-start(bf16[8,32,128]{2,1,0:T(8,128)(2,1)S(1)} %get-tuple-element.25), channel_id=1, source_target_pairs={{3,0},{0,1},{1,2},{2,3},{7,4},{4,5},{5,6},{6,7},{11,8},{8,9},{9,10... | collective-permute-start | bytes 196616 | tf_op jit(solution)/shard_map/ppermute | solution.py:23
  14.2 0.0 collective-permute-done.6.refs_2_
  14.2 2.3 %collective-permute-start.3 = (bf16[8,32,128]{2,1,0:T(8,128)(2,1)S(1)}, bf16[8,32,128]{2,1,0:T(8,128)(2,1)S(1)}, u32[]{:S(2)}, u32[]{:S(2)}) collective-permute-start(bf16[8,32,128]{2,1,0:T(8,128)(2,1)S(1)} %get-tuple-element.26), channel_id=1, source_target_pairs={{1,0},{2,1},{3,2},{0,3},{5,4},{6,5},{7,6},{4,7},{9,8},{10,9},{11,1... | collective-permute-start | bytes 196616 | tf_op jit(solution)/shard_map/ppermute | solution.py:23
  16.4 0.0 collective-permute-done.5.refs_1_
  16.4 0.0 collective-permute-done.4.refs_0_
  16.4 1.3 %far.1 = (f32[12,32,128]{2,1,0:T(8,128)S(1)}, bf16[12,32,128]{2,1,0:T(8,128)(2,1)S(1)}, bf16[12,32,128]{2,1,0:T(8,128)(2,1)S(1)}, bf16[12,32,128]{2,1,0:T(8,128)(2,1)S(1)}) custom-call(s32[32]{0:T(128)S(1)} %get-tuple-element.20.words, bf16[24,128,128]{2,1,0:T(8,128)(2,1)S(1)} %bitcast.3, bf16[2,128,128]{2,1,0:T(8,128)(2,1)S(1)} %get-tuple-element.21.flipped, ...), custom_call_target="tpu_custom_call" | custom-call | flops 200000000 | bytes 2000000 | tf_op jit(solution)/shard_map/far/pallas_call | solution.py:207
  17.7 0.1 collective-permute-start.7
  17.8 0.6 %collective-permute-start.8 = (bf16[12,32,128]{2,1,0:T(8,128)(2,1)S(1)}, bf16[12,32,128]{2,1,0:T(8,128)(2,1)S(1)}, u32[]{:S(2)}, u32[]{:S(2)}) collective-permute-start(bf16[12,32,128]{2,1,0:T(8,128)(2,1)S(1)} %get-tuple-element.33), channel_id=1, source_target_pairs={{3,0},{0,1},{1,2},{2,3},{7,4},{4,5},{5,6},{6,7},{11,8},{8,9},{9,10... | collective-permute-start | bytes 294920 | tf_op jit(solution)/shard_map/ppermute | solution.py:23
  18.4 0.0 collective-permute-done.1.refs_1_
  18.4 0.8 %collective-permute-done.2.refs_2_ = bf16[8,32,128]{2,1,0:T(8,128)(2,1)S(1)} collective-permute-done((bf16[8,32,128]{2,1,0:T(8,128)(2,1)S(1)}, bf16[8,32,128]{2,1,0:T(8,128)(2,1)S(1)}, u32[]{:S(2)}, u32[]{:S(2)}) %collective-permute-start.2) | collective-permute-done | bytes 65568 | tf_op jit(solution)/shard_map/ppermute | solution.py:23
  19.1 0.0 collective-permute-done.3.refs_3_
  19.1 4.0 %collective-permute-start.9 = (bf16[12,32,128]{2,1,0:T(8,128)(2,1)S(1)}, bf16[12,32,128]{2,1,0:T(8,128)(2,1)S(1)}, u32[]{:S(2)}, u32[]{:S(2)}) collective-permute-start(bf16[12,32,128]{2,1,0:T(8,128)(2,1)S(1)} %get-tuple-element.34), channel_id=1, source_target_pairs={{1,0},{2,1},{3,2},{0,3},{5,4},{6,5},{7,6},{4,7},{9,8},{10,9},{11,1... | collective-permute-start | bytes 294920 | tf_op jit(solution)/shard_map/ppermute | solution.py:23
  23.1 2.9 %collective-permute-done.7.refs_5_ = bf16[12,32,128]{2,1,0:T(8,128)(2,1)S(1)} collective-permute-done((bf16[12,32,128]{2,1,0:T(8,128)(2,1)S(1)}, bf16[12,32,128]{2,1,0:T(8,128)(2,1)S(1)}, u32[]{:S(2)}, u32[]{:S(2)}) %collective-permute-start.7) | collective-permute-done | bytes 98336 | tf_op jit(solution)/shard_map/ppermute | solution.py:23
  26.0 0.0 collective-permute-done.8.refs_6_
  26.0 0.0 collective-permute-done.9.refs_7_
  26.0 0.7 %finish.1 = f32[2,5,2,32,128]{4,3,2,1,0:T(8,128)} custom-call(f32[8,32,128]{2,1,0:T(8,128)S(1)} %get-tuple-element.23.refs_0_, bf16[8,32,128]{2,1,0:T(8,128)(2,1)S(1)} %collective-permute-done.1.refs_1_, bf16[8,32,128]{2,1,0:T(8,128)(2,1)S(1)} %collective-permute-done.2.refs_2_, bf16[8,32,128]{2,1,0:T(8,128)(2,1)S(1)} %collective-permute-done.3.refs_3_, ...), custom_call_target="tpu_custom_call" | custom-call | flops 1000000 | bytes 1500000 | tf_op jit(solution)/shard_map/finish/pallas_call | solution.py:254
Async XLA Ops:
  0.0 8.8 %copy-start = (bf16[2,12,128,128]{3,2,1,0:T(8,128)(2,1)S(1)}, bf16[2,12,128,128]{3,2,1,0:T(8,128)(2,1)}, u32[]{:S(2)}) copy-start(bf16[2,12,128,128]{3,2,1,0:T(8,128)(2,1)} %blocks.1) | copy-start | bytes 2359300
  2.7 6.1 %collective-permute-start = (bf16[2,128,128]{2,1,0:T(8,128)(2,1)S(1)}, bf16[2,128,128]{2,1,0:T(8,128)(2,1)S(1)}, u32[]{:S(2)}, u32[]{:S(2)}) collective-permute-start(bf16[2,128,128]{2,1,0:T(8,128)(2,1)S(1)} %get-tuple-element.22.refs_0_), channel_id=1, source_target_pairs={{4,0},{0,4},{12,8},{8,12},{20,16},{16,20},{28,24},{24,28},{5,1},{1... | collective-permute-start | bytes 196616 | tf_op jit(solution)/shard_map/ppermute | solution.py:28
  3.3 10.9 %collective-permute-start.6 = (bf16[2,128,128]{2,1,0:T(8,128)(2,1)S(1)}, bf16[2,128,128]{2,1,0:T(8,128)(2,1)S(1)}, u32[]{:S(2)}, u32[]{:S(2)}) collective-permute-start(bf16[2,128,128]{2,1,0:T(8,128)(2,1)S(1)} %get-tuple-element.22.refs_0_), channel_id=1, source_target_pairs={{28,0},{8,4},{4,8},{16,12},{12,16},{24,20},{20,24},{0,28},{29,1},{... | collective-permute-start | bytes 196616 | tf_op jit(solution)/shard_map/ppermute | solution.py:33
  6.8 9.6 %collective-permute-start.5 = (bf16[2,128,128]{2,1,0:T(8,128)(2,1)S(1)}, bf16[2,128,128]{2,1,0:T(8,128)(2,1)S(1)}, u32[]{:S(2)}, u32[]{:S(2)}) collective-permute-start(bf16[2,128,128]{2,1,0:T(8,128)(2,1)S(1)} %get-tuple-element.22.refs_0_), channel_id=1, source_target_pairs={{8,0},{12,4},{16,8},{20,12},{24,16},{28,20},{0,24},{4,28},{9,1},{1... | collective-permute-start | bytes 196616 | tf_op jit(solution)/shard_map/ppermute | solution.py:23
  7.3 9.1 %collective-permute-start.4 = (bf16[2,128,128]{2,1,0:T(8,128)(2,1)S(1)}, bf16[2,128,128]{2,1,0:T(8,128)(2,1)S(1)}, u32[]{:S(2)}, u32[]{:S(2)}) collective-permute-start(bf16[2,128,128]{2,1,0:T(8,128)(2,1)S(1)} %get-tuple-element.22.refs_0_), channel_id=1, source_target_pairs={{24,0},{28,4},{0,8},{4,12},{8,16},{12,20},{16,24},{20,28},{25,1},{... | collective-permute-start | bytes 196616 | tf_op jit(solution)/shard_map/ppermute | solution.py:23
  9.9 8.4 %collective-permute-start.1 = (bf16[8,32,128]{2,1,0:T(8,128)(2,1)S(1)}, bf16[8,32,128]{2,1,0:T(8,128)(2,1)S(1)}, u32[]{:S(2)}, u32[]{:S(2)}) collective-permute-start(bf16[8,32,128]{2,1,0:T(8,128)(2,1)S(1)} %get-tuple-element.24), channel_id=1, source_target_pairs={{2,0},{3,1},{0,2},{1,3},{6,4},{7,5},{4,6},{5,7},{10,8},{11,9},{8,1... | collective-permute-start | bytes 196616 | tf_op jit(solution)/shard_map/ppermute | solution.py:23
  12.6 6.5 %collective-permute-start.2 = (bf16[8,32,128]{2,1,0:T(8,128)(2,1)S(1)}, bf16[8,32,128]{2,1,0:T(8,128)(2,1)S(1)}, u32[]{:S(2)}, u32[]{:S(2)}) collective-permute-start(bf16[8,32,128]{2,1,0:T(8,128)(2,1)S(1)} %get-tuple-element.25), channel_id=1, source_target_pairs={{3,0},{0,1},{1,2},{2,3},{7,4},{4,5},{5,6},{6,7},{11,8},{8,9},{9,10... | collective-permute-start | bytes 196616 | tf_op jit(solution)/shard_map/ppermute | solution.py:23
  14.2 5.0 %collective-permute-start.3 = (bf16[8,32,128]{2,1,0:T(8,128)(2,1)S(1)}, bf16[8,32,128]{2,1,0:T(8,128)(2,1)S(1)}, u32[]{:S(2)}, u32[]{:S(2)}) collective-permute-start(bf16[8,32,128]{2,1,0:T(8,128)(2,1)S(1)} %get-tuple-element.26), channel_id=1, source_target_pairs={{1,0},{2,1},{3,2},{0,3},{5,4},{6,5},{7,6},{4,7},{9,8},{10,9},{11,1... | collective-permute-start | bytes 196616 | tf_op jit(solution)/shard_map/ppermute | solution.py:23
  17.7 8.3 %collective-permute-start.7 = (bf16[12,32,128]{2,1,0:T(8,128)(2,1)S(1)}, bf16[12,32,128]{2,1,0:T(8,128)(2,1)S(1)}, u32[]{:S(2)}, u32[]{:S(2)}) collective-permute-start(bf16[12,32,128]{2,1,0:T(8,128)(2,1)S(1)} %get-tuple-element.32), channel_id=1, source_target_pairs={{2,0},{3,1},{0,2},{1,3},{6,4},{7,5},{4,6},{5,7},{10,8},{11,9},{8,1... | collective-permute-start | bytes 294920 | tf_op jit(solution)/shard_map/ppermute | solution.py:23
  17.8 8.3 %collective-permute-start.8 = (bf16[12,32,128]{2,1,0:T(8,128)(2,1)S(1)}, bf16[12,32,128]{2,1,0:T(8,128)(2,1)S(1)}, u32[]{:S(2)}, u32[]{:S(2)}) collective-permute-start(bf16[12,32,128]{2,1,0:T(8,128)(2,1)S(1)} %get-tuple-element.33), channel_id=1, source_target_pairs={{3,0},{0,1},{1,2},{2,3},{7,4},{4,5},{5,6},{6,7},{11,8},{8,9},{9,10... | collective-permute-start | bytes 294920 | tf_op jit(solution)/shard_map/ppermute | solution.py:23
  19.1 6.9 %collective-permute-start.9 = (bf16[12,32,128]{2,1,0:T(8,128)(2,1)S(1)}, bf16[12,32,128]{2,1,0:T(8,128)(2,1)S(1)}, u32[]{:S(2)}, u32[]{:S(2)}) collective-permute-start(bf16[12,32,128]{2,1,0:T(8,128)(2,1)S(1)} %get-tuple-element.34), channel_id=1, source_target_pairs={{1,0},{2,1},{3,2},{0,3},{5,4},{6,5},{7,6},{4,7},{9,8},{10,9},{11,1... | collective-permute-start | bytes 294920 | tf_op jit(solution)/shard_map/ppermute | solution.py:23

commit v6 on v5

--- a/solution.py
+++ b/solution.py
@@ -21,6 +21,11 @@
 def from_behind(block, axis, distance):
     size = lax.axis_size(axis)
     return lax.ppermute(block, axis, [((i - distance) % size, i) for i in range(size)])
+
+
+def from_partner(block, distance):
+    size = lax.axis_size("grp")
+    return lax.ppermute(block, "grp", [(i ^ distance, i) for i in range(size)])
 
 
 def from_sibling(block):
@@ -187,7 +192,7 @@
         rows = out.shape[1]
         start = 0
         if parts > 1:
-            target = lax.rem(lax.axis_index("grp") + distance, parts)
+            target = (lax.rem(lax.axis_index("grp") + distance, parts)) if far else (lax.axis_index("grp") ^ distance)
             start = pl.multiple_of(target * rows, rows)
         skip = out.shape[0] - dests
         if carry:
@@ -278,20 +283,19 @@
     ahead = from_behind(own, "blk", -2)
     across = from_across(own)
 
-    split = parts <= 4
+    split = parts in ORDER
     share = parts if split else 1
     early = EARLY[parts] if split else []
-    late = LATE[parts] if split else []
+    late = []
     layout = [(0, False)] + [(d, False) for d in early + late]
     near = galerkin_call(False, layout, share, todo, blocks, flipped, [own, sibling], [])
     near_own, near_early, near_late = near[0], near[1 : 1 + len(early)], near[1 + len(early) :]
-    near_early = [from_behind(piece, "grp", d) for piece, d in zip(near_early, early)]
+    near_early = [from_partner(piece, d) for piece, d in zip(near_early, early)]
     layout = [(0, False)] + [(d, False) for d in early] + [(d, True) for d in late]
     far = galerkin_call(True, layout, share, todo, blocks, flipped, [behind, ahead, across], near_late)
     if near_early:
-        *far, last = far
-        near_early, last = lax.optimization_barrier((near_early, last))
-        far = [*far, last]
+        far, at = list(far), 1 + early.index(ORDER[parts][-1])
+        near_early, far[at] = lax.optimization_barrier((near_early, far[at]))
     far_own, far_early, both = far[0], far[1 : 1 + len(early)], far[1 + len(early) :]
     order = [d for d in ORDER[parts]] if split else []
     moved = {d: from_behind(piece, "grp", d) for d, piece in sorted(
@@ -305,9 +309,8 @@
     )
 
 
-EARLY = {1: [], 2: [1], 3: [1], 4: [2, 1, 3]}
-LATE = {1: [], 2: [], 3: [2], 4: []}
-ORDER = {1: [], 2: [1], 3: [1, 2], 4: [2, 1, 3]}
+EARLY = {1: [], 2: [1], 4: [2, 3, 1]}
+ORDER = {1: [], 2: [1], 4: [1, 2, 3]}
 
 
 def gathered(whole, parts):

time: 27.2 us -> 27 us (level)
    ppermute x8 -> x5, starting transfers between devices: 13.1 us -> 8.71 us  [from_behind(): lax.ppermute(block, axis, [((i - distance) % size, i) for i in range(size)])]
    ppermute x0 -> x3, starting transfers between devices: none -> 4.23 us  [from_partner(): return lax.ppermute(block, 'grp', [(i ^ distance, i) for i in range(size)])]
    ppermute x8 -> x5, waiting for transfers between devices: 3.7 us -> 3.33 us  [from_behind(): lax.ppermute(block, axis, [((i - distance) % size, i) for i in range(size)])]
    ppermute x0 -> x3, waiting for transfers between devices: none -> 0.36 us  [from_partner(): return lax.ppermute(block, 'grp', [(i ^ distance, i) for i in range(size)])]
  transfers between devices with their start and end apart: 10 -> 10, of which waited for: 2 -> 3; matrix products, arithmetic and copies ran while one was open for 0% -> 0% of each run, Pallas kernels for 9% -> 9%
where the time goes in v6:
time: 27 us; the launch traced here: 26.6 us
  starting transfers between devices  17 us (63%)
  Pallas kernels  5.09 us (19%)
  waiting for transfers between devices  3.7 us (14%)
  between operations  0.76 us (3%)
    ppermute x5, starting transfers between devices, from_behind(): lax.ppermute(block, axis, [((i - distance) % size, i) for i in range(size)])  8.71 us
    ppermute x3, starting transfers between devices, from_partner(): return lax.ppermute(block, 'grp', [(i ^ distance, i) for i in range(size)])  4.23 us
    ppermute x1, starting transfers between devices, from_across(): lax.ppermute(block, 'blk', [((i + (1 if i % 2 else -1)) % size, i) for i...  3.56 us
    ppermute x5, waiting for transfers between devices, from_behind(): lax.ppermute(block, axis, [((i - distance) % size, i) for i in range(size)])  3.33 us
    pallas_call x2, Pallas kernels, galerkin_call(): pl.pallas_call(functools.partial(galerkin_kernel, far, layout, parts, nnz...  2.37 us
    pallas_call x1, Pallas kernels, prolong_call(): pl.pallas_call(prolong_kernel, out_shape=(jax.ShapeDtypeStruct(tentative....  2 us
    pallas_call x1, Pallas kernels, finish_call(): pl.pallas_call(functools.partial(finish_kernel, len(near), len(far), len(...  0.73 us
  transfers between devices with their start and end apart: 10, of which 3 were waited for; matrix products, arithmetic and copies ran while one was open for 0% of the time, Pallas kernels for 9%

profile of v6, /device:TPU:0, one launch (start us, length us, event | category | flops | bytes accessed | tf_op | source)
XLA Modules:
  0.0 26.6 jit_solution(11618800187421555878)
XLA Ops:
  0.0 0.0 copy-start
  0.7 2.0 %prolong.1 = (bf16[2,128,128]{2,1,0:T(8,128)(2,1)S(1)}, bf16[2,128,128]{2,1,0:T(8,128)(2,1)S(1)}, s32[32]{0:T(128)S(1)}) custom-call(s32[1]{0:T(128)S(6)} %copy.7.counts, s32[2,12]{1,0:T(2,128)} %neighbours.1, s32[1,2,8]{2,1,0:T(2,128)} %bitcast.4, bf16[2,12,128,128]{3,2,1,0:T(8,128)(2,1)} %blocks.1, bf16[2,128,128]{2,1,0:T(8,128)(2,1)} %tentative.1, ...), custom_call_target="tpu_custom_call" | custom-call | flops 100000000 | bytes 1000000 | tf_op jit(solution)/shard_map/prolong/pallas_call | solution.py:122
  2.7 0.5 %collective-permute-start = (bf16[2,128,128]{2,1,0:T(8,128)(2,1)S(1)}, bf16[2,128,128]{2,1,0:T(8,128)(2,1)S(1)}, u32[]{:S(2)}, u32[]{:S(2)}) collective-permute-start(bf16[2,128,128]{2,1,0:T(8,128)(2,1)S(1)} %get-tuple-element.22.refs_0_), channel_id=1, source_target_pairs={{4,0},{0,4},{12,8},{8,12},{20,16},{16,20},{28,24},{24,28},{5,1},{1... | collective-permute-start | bytes 196616 | tf_op jit(solution)/shard_map/ppermute | solution.py:33
  3.3 3.6 %collective-permute-start.6 = (bf16[2,128,128]{2,1,0:T(8,128)(2,1)S(1)}, bf16[2,128,128]{2,1,0:T(8,128)(2,1)S(1)}, u32[]{:S(2)}, u32[]{:S(2)}) collective-permute-start(bf16[2,128,128]{2,1,0:T(8,128)(2,1)S(1)} %get-tuple-element.22.refs_0_), channel_id=1, source_target_pairs={{28,0},{8,4},{4,8},{16,12},{12,16},{24,20},{20,24},{0,28},{29,1},{... | collective-permute-start | bytes 196616 | tf_op jit(solution)/shard_map/ppermute | solution.py:38
  6.8 0.5 %collective-permute-start.5 = (bf16[2,128,128]{2,1,0:T(8,128)(2,1)S(1)}, bf16[2,128,128]{2,1,0:T(8,128)(2,1)S(1)}, u32[]{:S(2)}, u32[]{:S(2)}) collective-permute-start(bf16[2,128,128]{2,1,0:T(8,128)(2,1)S(1)} %get-tuple-element.22.refs_0_), channel_id=1, source_target_pairs={{8,0},{12,4},{16,8},{20,12},{24,16},{28,20},{0,24},{4,28},{9,1},{1... | collective-permute-start | bytes 196616 | tf_op jit(solution)/shard_map/ppermute | solution.py:23
  7.3 1.5 %collective-permute-start.4 = (bf16[2,128,128]{2,1,0:T(8,128)(2,1)S(1)}, bf16[2,128,128]{2,1,0:T(8,128)(2,1)S(1)}, u32[]{:S(2)}, u32[]{:S(2)}) collective-permute-start(bf16[2,128,128]{2,1,0:T(8,128)(2,1)S(1)} %get-tuple-element.22.refs_0_), channel_id=1, source_target_pairs={{24,0},{28,4},{0,8},{4,12},{8,16},{12,20},{16,24},{20,28},{25,1},{... | collective-permute-start | bytes 196616 | tf_op jit(solution)/shard_map/ppermute | solution.py:23
  8.8 0.0 collective-permute-done.refs_1_
  8.8 0.0 copy-done
  8.8 1.1 %near.1 = (f32[8,32,128]{2,1,0:T(8,128)S(1)}, bf16[8,32,128]{2,1,0:T(8,128)(2,1)S(1)}, bf16[8,32,128]{2,1,0:T(8,128)(2,1)S(1)}, bf16[8,32,128]{2,1,0:T(8,128)(2,1)S(1)}) custom-call(s32[32]{0:T(128)S(1)} %get-tuple-element.20.words, bf16[24,128,128]{2,1,0:T(8,128)(2,1)S(1)} %bitcast.2, bf16[2,128,128]{2,1,0:T(8,128)(2,1)S(1)} %get-tuple-element.21.flipped, ...), custom_call_target="tpu_custom_call" | custom-call | flops 200000000 | bytes 2000000 | tf_op jit(solution)/shard_map/near/pallas_call | solution.py:212
  9.9 2.7 %collective-permute-start.1 = (bf16[8,32,128]{2,1,0:T(8,128)(2,1)S(1)}, bf16[8,32,128]{2,1,0:T(8,128)(2,1)S(1)}, u32[]{:S(2)}, u32[]{:S(2)}) collective-permute-start(bf16[8,32,128]{2,1,0:T(8,128)(2,1)S(1)} %get-tuple-element.24), channel_id=1, source_target_pairs={{2,0},{3,1},{0,2},{1,3},{6,4},{7,5},{4,6},{5,7},{10,8},{11,9},{8,1... | collective-permute-start | bytes 196616 | tf_op jit(solution)/shard_map/ppermute | solution.py:28
  12.6 1.3 %collective-permute-start.2 = (bf16[8,32,128]{2,1,0:T(8,128)(2,1)S(1)}, bf16[8,32,128]{2,1,0:T(8,128)(2,1)S(1)}, u32[]{:S(2)}, u32[]{:S(2)}) collective-permute-start(bf16[8,32,128]{2,1,0:T(8,128)(2,1)S(1)} %get-tuple-element.25), channel_id=1, source_target_pairs={{3,0},{2,1},{1,2},{0,3},{7,4},{6,5},{5,6},{4,7},{11,8},{10,9},{9,1... | collective-permute-start | bytes 196616 | tf_op jit(solution)/shard_map/ppermute | solution.py:28
  13.9 0.0 collective-permute-done.6.refs_2_
  13.9 0.2 collective-permute-start.3
  14.2 0.0 collective-permute-done.5.refs_1_
  14.2 0.0 collective-permute-done.4.refs_0_
  14.2 1.3 %far.1 = (f32[12,32,128]{2,1,0:T(8,128)S(1)}, bf16[12,32,128]{2,1,0:T(8,128)(2,1)S(1)}, bf16[12,32,128]{2,1,0:T(8,128)(2,1)S(1)}, bf16[12,32,128]{2,1,0:T(8,128)(2,1)S(1)}) custom-call(s32[32]{0:T(128)S(1)} %get-tuple-element.20.words, bf16[24,128,128]{2,1,0:T(8,128)(2,1)S(1)} %bitcast.3, bf16[2,128,128]{2,1,0:T(8,128)(2,1)S(1)} %get-tuple-element.21.flipped, ...), custom_call_target="tpu_custom_call" | custom-call | flops 200000000 | bytes 2000000 | tf_op jit(solution)/shard_map/far/pallas_call | solution.py:212
  15.5 2.9 %collective-permute-start.7 = (bf16[12,32,128]{2,1,0:T(8,128)(2,1)S(1)}, bf16[12,32,128]{2,1,0:T(8,128)(2,1)S(1)}, u32[]{:S(2)}, u32[]{:S(2)}) collective-permute-start(bf16[12,32,128]{2,1,0:T(8,128)(2,1)S(1)} %get-tuple-element.32), channel_id=1, source_target_pairs={{2,0},{3,1},{0,2},{1,3},{6,4},{7,5},{4,6},{5,7},{10,8},{11,9},{8,1... | collective-permute-start | bytes 294920 | tf_op jit(solution)/shard_map/ppermute | solution.py:23
  18.3 0.7 %collective-permute-start.9 = (bf16[12,32,128]{2,1,0:T(8,128)(2,1)S(1)}, bf16[12,32,128]{2,1,0:T(8,128)(2,1)S(1)}, u32[]{:S(2)}, u32[]{:S(2)}) collective-permute-start(bf16[12,32,128]{2,1,0:T(8,128)(2,1)S(1)} %get-tuple-element.34), channel_id=1, source_target_pairs={{3,0},{0,1},{1,2},{2,3},{7,4},{4,5},{5,6},{6,7},{11,8},{8,9},{9,10... | collective-permute-start | bytes 294920 | tf_op jit(solution)/shard_map/ppermute | solution.py:23
  19.0 0.0 collective-permute-done.1.refs_1_
  19.0 0.4 %collective-permute-done.2.refs_2_ = bf16[8,32,128]{2,1,0:T(8,128)(2,1)S(1)} collective-permute-done((bf16[8,32,128]{2,1,0:T(8,128)(2,1)S(1)}, bf16[8,32,128]{2,1,0:T(8,128)(2,1)S(1)}, u32[]{:S(2)}, u32[]{:S(2)}) %collective-permute-start.2) | collective-permute-done | bytes 65568 | tf_op jit(solution)/shard_map/ppermute | solution.py:28
  19.4 0.0 collective-permute-done.3.refs_3_
  19.4 3.1 %collective-permute-start.8 = (bf16[12,32,128]{2,1,0:T(8,128)(2,1)S(1)}, bf16[12,32,128]{2,1,0:T(8,128)(2,1)S(1)}, u32[]{:S(2)}, u32[]{:S(2)}) collective-permute-start(bf16[12,32,128]{2,1,0:T(8,128)(2,1)S(1)} %get-tuple-element.33), channel_id=1, source_target_pairs={{1,0},{2,1},{3,2},{0,3},{5,4},{6,5},{7,6},{4,7},{9,8},{10,9},{11,1... | collective-permute-start | bytes 294920 | tf_op jit(solution)/shard_map/ppermute | solution.py:23
  22.5 3.2 %collective-permute-done.7.refs_5_ = bf16[12,32,128]{2,1,0:T(8,128)(2,1)S(1)} collective-permute-done((bf16[12,32,128]{2,1,0:T(8,128)(2,1)S(1)}, bf16[12,32,128]{2,1,0:T(8,128)(2,1)S(1)}, u32[]{:S(2)}, u32[]{:S(2)}) %collective-permute-start.7) | collective-permute-done | bytes 98336 | tf_op jit(solution)/shard_map/ppermute | solution.py:23
  25.7 0.0 collective-permute-done.9.refs_7_
  25.7 0.2 collective-permute-done.8.refs_6_
  25.8 0.7 %finish.1 = f32[2,5,2,32,128]{4,3,2,1,0:T(8,128)} custom-call(f32[8,32,128]{2,1,0:T(8,128)S(1)} %get-tuple-element.23.refs_0_, bf16[8,32,128]{2,1,0:T(8,128)(2,1)S(1)} %collective-permute-done.1.refs_1_, bf16[8,32,128]{2,1,0:T(8,128)(2,1)S(1)} %collective-permute-done.2.refs_2_, bf16[8,32,128]{2,1,0:T(8,128)(2,1)S(1)} %collective-permute-done.3.refs_3_, ...), custom_call_target="tpu_custom_call" | custom-call | flops 1000000 | bytes 1500000 | tf_op jit(solution)/shard_map/finish/pallas_call | solution.py:259
Async XLA Ops:
  0.0 8.8 %copy-start = (bf16[2,12,128,128]{3,2,1,0:T(8,128)(2,1)S(1)}, bf16[2,12,128,128]{3,2,1,0:T(8,128)(2,1)}, u32[]{:S(2)}) copy-start(bf16[2,12,128,128]{3,2,1,0:T(8,128)(2,1)} %blocks.1) | copy-start | bytes 2359300
  2.7 6.1 %collective-permute-start = (bf16[2,128,128]{2,1,0:T(8,128)(2,1)S(1)}, bf16[2,128,128]{2,1,0:T(8,128)(2,1)S(1)}, u32[]{:S(2)}, u32[]{:S(2)}) collective-permute-start(bf16[2,128,128]{2,1,0:T(8,128)(2,1)S(1)} %get-tuple-element.22.refs_0_), channel_id=1, source_target_pairs={{4,0},{0,4},{12,8},{8,12},{20,16},{16,20},{28,24},{24,28},{5,1},{1... | collective-permute-start | bytes 196616 | tf_op jit(solution)/shard_map/ppermute | solution.py:33
  3.3 10.7 %collective-permute-start.6 = (bf16[2,128,128]{2,1,0:T(8,128)(2,1)S(1)}, bf16[2,128,128]{2,1,0:T(8,128)(2,1)S(1)}, u32[]{:S(2)}, u32[]{:S(2)}) collective-permute-start(bf16[2,128,128]{2,1,0:T(8,128)(2,1)S(1)} %get-tuple-element.22.refs_0_), channel_id=1, source_target_pairs={{28,0},{8,4},{4,8},{16,12},{12,16},{24,20},{20,24},{0,28},{29,1},{... | collective-permute-start | bytes 196616 | tf_op jit(solution)/shard_map/ppermute | solution.py:38
  6.8 7.4 %collective-permute-start.5 = (bf16[2,128,128]{2,1,0:T(8,128)(2,1)S(1)}, bf16[2,128,128]{2,1,0:T(8,128)(2,1)S(1)}, u32[]{:S(2)}, u32[]{:S(2)}) collective-permute-start(bf16[2,128,128]{2,1,0:T(8,128)(2,1)S(1)} %get-tuple-element.22.refs_0_), channel_id=1, source_target_pairs={{8,0},{12,4},{16,8},{20,12},{24,16},{28,20},{0,24},{4,28},{9,1},{1... | collective-permute-start | bytes 196616 | tf_op jit(solution)/shard_map/ppermute | solution.py:23
  7.3 6.8 %collective-permute-start.4 = (bf16[2,128,128]{2,1,0:T(8,128)(2,1)S(1)}, bf16[2,128,128]{2,1,0:T(8,128)(2,1)S(1)}, u32[]{:S(2)}, u32[]{:S(2)}) collective-permute-start(bf16[2,128,128]{2,1,0:T(8,128)(2,1)S(1)} %get-tuple-element.22.refs_0_), channel_id=1, source_target_pairs={{24,0},{28,4},{0,8},{4,12},{8,16},{12,20},{16,24},{20,28},{25,1},{... | collective-permute-start | bytes 196616 | tf_op jit(solution)/shard_map/ppermute | solution.py:23
  9.9 9.1 %collective-permute-start.1 = (bf16[8,32,128]{2,1,0:T(8,128)(2,1)S(1)}, bf16[8,32,128]{2,1,0:T(8,128)(2,1)S(1)}, u32[]{:S(2)}, u32[]{:S(2)}) collective-permute-start(bf16[8,32,128]{2,1,0:T(8,128)(2,1)S(1)} %get-tuple-element.24), channel_id=1, source_target_pairs={{2,0},{3,1},{0,2},{1,3},{6,4},{7,5},{4,6},{5,7},{10,8},{11,9},{8,1... | collective-permute-start | bytes 196616 | tf_op jit(solution)/shard_map/ppermute | solution.py:28
  12.6 6.8 %collective-permute-start.2 = (bf16[8,32,128]{2,1,0:T(8,128)(2,1)S(1)}, bf16[8,32,128]{2,1,0:T(8,128)(2,1)S(1)}, u32[]{:S(2)}, u32[]{:S(2)}) collective-permute-start(bf16[8,32,128]{2,1,0:T(8,128)(2,1)S(1)} %get-tuple-element.25), channel_id=1, source_target_pairs={{3,0},{2,1},{1,2},{0,3},{7,4},{6,5},{5,6},{4,7},{11,8},{10,9},{9,1... | collective-permute-start | bytes 196616 | tf_op jit(solution)/shard_map/ppermute | solution.py:28
  13.9 5.5 %collective-permute-start.3 = (bf16[8,32,128]{2,1,0:T(8,128)(2,1)S(1)}, bf16[8,32,128]{2,1,0:T(8,128)(2,1)S(1)}, u32[]{:S(2)}, u32[]{:S(2)}) collective-permute-start(bf16[8,32,128]{2,1,0:T(8,128)(2,1)S(1)} %get-tuple-element.26), channel_id=1, source_target_pairs={{1,0},{0,1},{3,2},{2,3},{5,4},{4,5},{7,6},{6,7},{9,8},{8,9},{11,10... | collective-permute-start | bytes 196616 | tf_op jit(solution)/shard_map/ppermute | solution.py:28
  15.5 10.2 %collective-permute-start.7 = (bf16[12,32,128]{2,1,0:T(8,128)(2,1)S(1)}, bf16[12,32,128]{2,1,0:T(8,128)(2,1)S(1)}, u32[]{:S(2)}, u32[]{:S(2)}) collective-permute-start(bf16[12,32,128]{2,1,0:T(8,128)(2,1)S(1)} %get-tuple-element.32), channel_id=1, source_target_pairs={{2,0},{3,1},{0,2},{1,3},{6,4},{7,5},{4,6},{5,7},{10,8},{11,9},{8,1... | collective-permute-start | bytes 294920 | tf_op jit(solution)/shard_map/ppermute | solution.py:23
  18.3 7.3 %collective-permute-start.9 = (bf16[12,32,128]{2,1,0:T(8,128)(2,1)S(1)}, bf16[12,32,128]{2,1,0:T(8,128)(2,1)S(1)}, u32[]{:S(2)}, u32[]{:S(2)}) collective-permute-start(bf16[12,32,128]{2,1,0:T(8,128)(2,1)S(1)} %get-tuple-element.34), channel_id=1, source_target_pairs={{3,0},{0,1},{1,2},{2,3},{7,4},{4,5},{5,6},{6,7},{11,8},{8,9},{9,10... | collective-permute-start | bytes 294920 | tf_op jit(solution)/shard_map/ppermute | solution.py:23
  19.4 6.5 %collective-permute-start.8 = (bf16[12,32,128]{2,1,0:T(8,128)(2,1)S(1)}, bf16[12,32,128]{2,1,0:T(8,128)(2,1)S(1)}, u32[]{:S(2)}, u32[]{:S(2)}) collective-permute-start(bf16[12,32,128]{2,1,0:T(8,128)(2,1)S(1)} %get-tuple-element.33), channel_id=1, source_target_pairs={{1,0},{2,1},{3,2},{0,3},{5,4},{6,5},{7,6},{4,7},{9,8},{10,9},{11,1... | collective-permute-start | bytes 294920 | tf_op jit(solution)/shard_map/ppermute | solution.py:23
